TPU v7x, 32 devices: a whole 2x2x4 slice. The times are simulated.
32 devices in a mesh: fsdp: 8 (over z, x), rep: 4 (over y, core).
Axes of the slice: x: 2, y: 2, z: 4, core: 2. Of those that a mesh axis runs over, the one named last changes fastest.
Arguments:
- video_in: bfloat16 [32, 196, 1024], P(('fsdp', 'rep')), may hold values from -6 to 6
- audio_in: bfloat16 [32, 128, 1024], P(('fsdp', 'rep')), may hold values from -6 to 6
- bottle_in: bfloat16 [32, 8, 1024], P(('fsdp', 'rep')), may hold values from -6 to 6
- video_gain: float32 [1024], replicated, may hold values from 0.5 to 8
- audio_gain: float32 [1024], replicated, may hold values from 0.5 to 8
- video_qkv: bfloat16 [1024, 3072], P('fsdp'), may hold values from -0.18 to 0.18
- video_out: bfloat16 [1024, 1024], P('fsdp'), may hold values from -0.1875 to 0.1875
- audio_qkv: bfloat16 [1024, 3072], P('fsdp'), may hold values from -0.18 to 0.18
- audio_out: bfloat16 [1024, 1024], P('fsdp'), may hold values from -0.1875 to 0.1875
- grad_video: bfloat16 [32, 196, 1024], P(('fsdp', 'rep')), may hold values from -6 to 6
- grad_audio: bfloat16 [32, 128, 1024], P(('fsdp', 'rep')), may hold values from -6 to 6
- grad_bottle: bfloat16 [32, 8, 1024], P(('fsdp', 'rep')), may hold values from -6 to 6
Outputs:
- dvideo_in: bfloat16 [32, 196, 1024], P(('fsdp', 'rep'))
- daudio_in: bfloat16 [32, 128, 1024], P(('fsdp', 'rep'))
- dbottle_in: bfloat16 [32, 8, 1024], P(('fsdp', 'rep'))
- video_qkv_grad: float32 [1024, 3072], P('fsdp')
- video_out_grad: float32 [1024, 1024], P('fsdp')
- audio_qkv_grad: float32 [1024, 3072], P('fsdp')
- audio_out_grad: float32 [1024, 1024], P('fsdp')
- video_gain_grad: float32 [1024], replicated
- audio_gain_grad: float32 [1024], replicated
All inputs are finite; a program needn't handle non-finite values.
Results may differ from a plain program's by a relative error of at most 0.025.
Values may be sent and summed in bfloat16 or wider, within the bound.
A program may use at most 128 MiB of HBM per device.

v0:
```python
import jax
import jax.numpy as jnp
from jax import lax
from jax.sharding import PartitionSpec as P

HEAD = 64


def stream(tokens, bottle, gain, w_qkv, w_out, d_tokens, bottle_half):
    f32 = jnp.float32
    bf16 = jnp.bfloat16
    z_rows = jnp.concatenate([tokens, bottle], 0)
    rows = z_rows.shape[0]
    width = z_rows.shape[1]
    zf = z_rows.astype(f32)
    inverse = lax.rsqrt(jnp.mean(zf * zf, axis=1, keepdims=True) + 1e-06)
    normed = zf * inverse
    hidden = (normed * gain).astype(bf16)
    qkv = jnp.dot(hidden, w_qkv, preferred_element_type=f32).astype(bf16)
    scale = HEAD ** (-0.5)
    query = qkv[:, :width].reshape(rows, -1, HEAD)
    keyed = qkv[:, width : 2 * width].reshape(rows, -1, HEAD)
    valued = qkv[:, 2 * width :].reshape(rows, -1, HEAD)
    scores = jnp.einsum("shd,thd->hst", query, keyed, preferred_element_type=f32) * scale
    probs = jax.nn.softmax(scores, axis=-1)
    pb = probs.astype(bf16)
    att = (
        jnp.einsum("hst,thd->shd", pb, valued, preferred_element_type=f32)
        .reshape(rows, width)
        .astype(bf16)
    )
    d_out = jnp.concatenate([d_tokens.astype(f32), bottle_half], 0)
    dyb = d_out.astype(bf16)
    out_term = jnp.einsum("sd,se->de", att, dyb, preferred_element_type=f32)
    datt = jnp.einsum("se,de->sd", dyb, w_out, preferred_element_type=f32).astype(bf16)
    datt = datt.reshape(rows, -1, HEAD)
    dprob = jnp.einsum("shd,thd->hst", datt, valued, preferred_element_type=f32)
    dvalue = jnp.einsum("hst,shd->thd", pb, datt, preferred_element_type=f32)
    dscore = probs * (dprob - jnp.sum(probs * dprob, axis=-1, keepdims=True)) * scale
    dsb = dscore.astype(bf16)
    dquery = jnp.einsum("hst,thd->shd", dsb, keyed, preferred_element_type=f32)
    dkey = jnp.einsum("hst,shd->thd", dsb, query, preferred_element_type=f32)
    dqkv = jnp.concatenate(
        [dquery.reshape(rows, width), dkey.reshape(rows, width), dvalue.reshape(rows, width)], 1
    ).astype(bf16)
    qkv_term = jnp.einsum("sd,se->de", hidden, dqkv, preferred_element_type=f32)
    dhidden = jnp.einsum("se,de->sd", dqkv, w_qkv, preferred_element_type=f32)
    gain_term = jnp.sum(dhidden * normed, axis=0)
    dnorm = dhidden * gain
    d_z = d_out + inverse * (dnorm - normed * jnp.mean(dnorm * normed, axis=1, keepdims=True))
    return (d_z, qkv_term, out_term, gain_term)


def all_clips(tokens, bottles, gain, w_qkv, w_out, d_tokens, d_bottles):

    def one_clip(carry, item):
        tok, bot, dtok, dbot = item
        half = dbot.astype(jnp.float32) * 0.5
        d_z, qkv_term, out_term, gain_term = stream(tok, bot, gain, w_qkv, w_out, dtok, half)
        return ((carry[0] + qkv_term, carry[1] + out_term, carry[2] + gain_term), d_z)

    width = w_out.shape[0]
    start = (
        jnp.zeros(w_qkv.shape, jnp.float32),
        jnp.zeros(w_out.shape, jnp.float32),
        jnp.zeros((width,), jnp.float32),
    )
    return lax.scan(one_clip, start, (tokens, bottles, d_tokens, d_bottles))


def fetch(qkv_shard, out_shard):
    groups = lax.axis_size("rep")
    place = lax.axis_index("rep")
    qkv_cols = qkv_shard.shape[1] // groups
    out_cols = out_shard.shape[1] // groups
    qkv_part = lax.dynamic_slice_in_dim(qkv_shard, place * qkv_cols, qkv_cols, 1)
    out_part = lax.dynamic_slice_in_dim(out_shard, place * out_cols, out_cols, 1)
    qkv_part, out_part = (
        lax.all_gather(qkv_part, "fsdp", axis=0, tiled=True),
        lax.all_gather(out_part, "fsdp", axis=0, tiled=True),
    )
    return (
        lax.all_gather(qkv_part, "rep", axis=1, tiled=True),
        lax.all_gather(out_part, "rep", axis=1, tiled=True),
    )


def reduce_grads(qkv_term, out_term, count):
    qkv_sum, out_sum = (
        lax.psum_scatter(
            qkv_term.astype(jnp.bfloat16), "rep", scatter_dimension=1, tiled=True
        ).astype(jnp.float32),
        lax.psum_scatter(
            out_term.astype(jnp.bfloat16), "rep", scatter_dimension=1, tiled=True
        ).astype(jnp.float32),
    )
    qkv_sum, out_sum = (
        lax.psum_scatter(
            qkv_sum.astype(jnp.bfloat16), "fsdp", scatter_dimension=0, tiled=True
        ).astype(jnp.float32),
        lax.psum_scatter(
            out_sum.astype(jnp.bfloat16), "fsdp", scatter_dimension=0, tiled=True
        ).astype(jnp.float32),
    )
    qkv_sum, out_sum = (
        lax.all_gather(qkv_sum.astype(jnp.bfloat16), "rep", axis=1, tiled=True).astype(
            qkv_sum.dtype
        ),
        lax.all_gather(out_sum.astype(jnp.bfloat16), "rep", axis=1, tiled=True).astype(
            out_sum.dtype
        ),
    )
    return (qkv_sum / count, out_sum / count)


def per_device(
    video_in,
    audio_in,
    bottle_in,
    video_gain,
    audio_gain,
    video_qkv,
    video_out,
    audio_qkv,
    audio_out,
    grad_video,
    grad_audio,
    grad_bottle,
):
    count = float(video_in.shape[0] * lax.axis_size("fsdp") * lax.axis_size("rep"))
    video_full, video_proj = fetch(video_qkv, video_out)
    video_sums, dz_video = all_clips(
        video_in, bottle_in, video_gain, video_full, video_proj, grad_video, grad_bottle
    )
    audio_full, audio_proj = fetch(audio_qkv, audio_out)
    video_qkv_grad, video_out_grad = reduce_grads(video_sums[0], video_sums[1], count)
    audio_sums, dz_audio = all_clips(
        audio_in, bottle_in, audio_gain, audio_full, audio_proj, grad_audio, grad_bottle
    )
    audio_qkv_grad, audio_out_grad = reduce_grads(audio_sums[0], audio_sums[1], count)
    gain_video, gain_audio = lax.psum((video_sums[2], audio_sums[2]), ("fsdp", "rep"))
    video_len = video_in.shape[1]
    audio_len = audio_in.shape[1]
    dvideo_in = dz_video[:, :video_len].astype(jnp.bfloat16)
    daudio_in = dz_audio[:, :audio_len].astype(jnp.bfloat16)
    dbottle_in = (dz_video[:, video_len:] + dz_audio[:, audio_len:]).astype(jnp.bfloat16)
    return (
        dvideo_in,
        daudio_in,
        dbottle_in,
        video_qkv_grad,
        video_out_grad,
        audio_qkv_grad,
        audio_out_grad,
        gain_video / count,
        gain_audio / count,
    )


def solution(mesh):
    in_specs = (
        P(("fsdp", "rep"), None, None),
        P(("fsdp", "rep"), None, None),
        P(("fsdp", "rep"), None, None),
        P(),
        P(),
        P("fsdp", None),
        P("fsdp", None),
        P("fsdp", None),
        P("fsdp", None),
        P(("fsdp", "rep"), None, None),
        P(("fsdp", "rep"), None, None),
        P(("fsdp", "rep"), None, None),
    )
    out_specs = (
        P(("fsdp", "rep"), None, None),
        P(("fsdp", "rep"), None, None),
        P(("fsdp", "rep"), None, None),
        P("fsdp", None),
        P("fsdp", None),
        P("fsdp", None),
        P("fsdp", None),
        P(),
        P(),
    )
    return jax.shard_map(
        per_device, mesh=mesh, in_specs=in_specs, out_specs=out_specs, check_vma=False
    )
```

profile of v0, /device:TPU:13, one launch (start us, length us, event | category | flops | bytes accessed | tf_op | source)
XLA Modules:
  0.0 714.7 jit_solution(1365999617299398199)
XLA Ops:
  7.2 1.1 copy-done
  8.3 0.7 constant_dynamic-slice_fusion.3
  9.1 1.6 constant_dynamic-slice_fusion.1
  10.8 44.1 %all-gather.7.cloned.1.call-done = bf16[1024,768]{1,0:T(8,128)(2,1)} async-done(((bf16[128,768]{1,0:T(8,128)(2,1)}), bf16[1024,768]{1,0:T(8,128)(2,1)}) %all-gather.7.cloned.1.call-update) | async-done | bytes 1572880 | tf_op jit(solution)/shard_map/all_gather | solution.py:79
  54.9 45.2 %all-gather.13.cloned.1.call-done = bf16[1024,768]{1,0:T(8,128)(2,1)} async-done(((bf16[128,768]{1,0:T(8,128)(2,1)}), bf16[1024,768]{1,0:T(8,128)(2,1)}) %all-gather.13.cloned.1.call-update) | async-done | bytes 1572880 | tf_op jit(solution)/shard_map/all_gather | solution.py:79
  100.3 0.9 constant_dynamic-slice_fusion.2
  101.2 25.4 %all_gather.38 = bf16[1024,256]{1,0:T(8,128)(2,1)} all-gather(bf16[128,256]{1,0:T(8,128)(2,1)S(1)} %constant_dynamic-slice_fusion.2), channel_id=1, replica_groups=mesh['fsdp'=8,'rep'=4] {'fsdp'}, dimensions={0}, use_global_device_ids=true | all-gather | bytes 589824 | tf_op jit(solution)/shard_map/all_gather | solution.py:80
  126.6 0.9 constant_dynamic-slice_fusion
  127.5 26.8 %all_gather.42 = bf16[1024,256]{1,0:T(8,128)(2,1)} all-gather(bf16[128,256]{1,0:T(8,128)(2,1)S(1)} %constant_dynamic-slice_fusion), channel_id=1, replica_groups=mesh['fsdp'=8,'rep'=4] {'fsdp'}, dimensions={0}, use_global_device_ids=true | all-gather | bytes 589824 | tf_op jit(solution)/shard_map/all_gather | solution.py:80
  154.7 5.0 convolution_convert_fusion.2
  159.8 0.2 copy.46
  160.0 0.2 copy.45
  160.3 0.2 copy.48
  160.5 3.1 fusion.111
  163.6 2.5 convolution_convert_fusion.8
  166.1 2.1 convolution_convert_fusion.5
  168.4 26.6 %all-gather.15.cloned.1.call-done = bf16[1024,3072]{1,0:T(8,128)(2,1)} async-done(((bf16[1024,768]{1,0:T(8,128)(2,1)}), bf16[1024,3072]{1,0:T(8,128)(2,1)}) %all-gather.15.cloned.1.call-update) | async-done | bytes 6291472 | tf_op jit(solution)/shard_map/all_gather | solution.py:83
  195.0 3.9 convolution_convert_fusion.3
  199.0 1.0 copy.74
  200.4 3.3 fusion.112
  203.8 2.1 convolution_convert_fusion.6
  205.9 2.0 convolution_convert_fusion.4
  207.9 0.2 reduce-scatter.9.cloned.1.call-start
  208.2 11.1 %all-gather.11.cloned.1.call-done = bf16[1024,1024]{1,0:T(8,128)(2,1)} async-done(((bf16[1024,256]{1,0:T(8,128)(2,1)}), bf16[1024,1024]{1,0:T(8,128)(2,1)}) %all-gather.11.cloned.1.call-update) | async-done | bytes 2097168 | tf_op jit(solution)/shard_map/all_gather | solution.py:84
  219.3 2.4 convolution_convert_fusion.10
  221.9 2.4 fusion.113
  224.3 7.4 %fusion.40 = bf16[16,64,204]{2,1,0:T(8,128)(2,1)} fusion(bf16[204,16,64]{0,2,1:T(8,128)(2,1)} %bitcast.95, f32[16,204,204]{1,2,0:T(8,128)} %fusion.113, f32[16,204,204]{1,2,0:T(8,128)} %get-tuple-element.82, f32[16,204]{1,0:T(8,128)S(1)} %get-tuple-element.81), kind=kOutput, calls=%fused_computation.37 | convolution fusion | flops 90102920 | bytes 6175488 | tf_op jit(solution)/shard_map/while/body/eval_jaxpr/hst,shd->thd/dot_general | solution.py:42
  231.8 6.9 fusion.37
  238.6 2.7 convolution_convert_fusion.9
  241.4 0.8 copy-done.23
  242.2 4.6 convolution_convert_fusion.1
  246.9 2.4 convolution_convert_fusion.11
  249.5 1.9 fusion.114
  251.5 6.2 fusion.34
  257.6 5.4 fusion.31
  263.0 2.5 convolution_convert_fusion.7
  265.6 0.8 copy-done.25
  266.4 4.6 convolution_convert_fusion
  271.0 5.6 reduce-scatter.13.cloned.1.call-done
  276.7 33.6 %reduce-scatter.21.cloned.1.call-done = bf16[1024,256]{1,0:T(8,128)(2,1)} async-done(((bf16[1024,1024]{1,0:T(8,128)(2,1)}), bf16[1024,256]{1,0:T(8,128)(2,1)}) %reduce-scatter.21.cloned.1.call-update) | async-done | bytes 524304 | tf_op jit(solution)/shard_map/reduce_scatter | solution.py:93
  310.4 60.4 %reduce-scatter.9.cloned.1.call-done = bf16[1024,768]{1,0:T(8,128)(2,1)} async-done(((bf16[1024,3072]{1,0:T(8,128)(2,1)}), bf16[1024,768]{1,0:T(8,128)(2,1)}) %reduce-scatter.9.cloned.1.call-update) | async-done | bytes 1572880 | tf_op jit(solution)/shard_map/reduce_scatter | solution.py:90
  370.9 0.3 reduce-scatter.19.cloned.1.call-start
  371.1 5.5 fusion.56
  376.6 0.3 fusion.55
  376.9 0.8 slice.64
  377.7 53.4 %reduce-scatter.17.cloned.1.call-done = bf16[1024,768]{1,0:T(8,128)(2,1)} async-done(((bf16[1024,3072]{1,0:T(8,128)(2,1)}), bf16[1024,768]{1,0:T(8,128)(2,1)}) %reduce-scatter.17.cloned.1.call-update) | async-done | bytes 1572880 | tf_op jit(solution)/shard_map/reduce_scatter | solution.py:90
  431.2 5.5 fusion.73
  436.7 0.2 fusion.72
  436.9 0.7 slice.65
  437.7 40.4 %all-reduce = (f32[1024]{0:T(1024)S(1)}, f32[1024]{0:T(1024)S(1)}) all-reduce(f32[1024]{0:T(1024)S(1)} %get-tuple-element.57, f32[1024]{0:T(1024)S(1)} %get-tuple-element.59), channel_id=1, replica_groups=mesh['fsdp'=8,'rep'=4] {'fsdp','rep'}, use_global_device_ids=true, to_apply=%region_19.20 | all-reduce | flops 2048 | bytes 16384 | tf_op jit(solution)/shard_map/psum | solution.py:141
  478.1 0.6 broadcast_multiply_fusion
  478.7 0.6 fusion.90
  479.3 16.7 %reduce-scatter.15.cloned.1.call-done = bf16[128,256]{1,0:T(8,128)(2,1)} async-done(((bf16[1024,256]{1,0:T(8,128)(2,1)}), bf16[128,256]{1,0:T(8,128)(2,1)}) %reduce-scatter.15.cloned.1.call-update) | async-done | bytes 65552 | tf_op jit(solution)/shard_map/reduce_scatter | solution.py:101
  496.0 8.6 %all_gather.45 = bf16[128,1024]{1,0:T(8,128)(2,1)S(1)} all-gather(bf16[128,256]{1,0:T(8,128)(2,1)} %reduce-scatter.15.cloned.1.call-done), channel_id=1, replica_groups=mesh['fsdp'=8,'rep'=4] {'rep'}, dimensions={1}, use_global_device_ids=true | all-gather | bytes 327680 | tf_op jit(solution)/shard_map/all_gather | solution.py:109
  504.6 56.2 %reduce-scatter.23.cloned.1.call-done = bf16[128,256]{1,0:T(8,128)(2,1)} async-done(((bf16[1024,256]{1,0:T(8,128)(2,1)}), bf16[128,256]{1,0:T(8,128)(2,1)}) %reduce-scatter.23.cloned.1.call-update) | async-done | bytes 65552 | tf_op jit(solution)/shard_map/reduce_scatter | solution.py:101
  560.8 8.6 %all_gather.47 = bf16[128,1024]{1,0:T(8,128)(2,1)S(1)} all-gather(bf16[128,256]{1,0:T(8,128)(2,1)} %reduce-scatter.23.cloned.1.call-done), channel_id=1, replica_groups=mesh['fsdp'=8,'rep'=4] {'rep'}, dimensions={1}, use_global_device_ids=true | all-gather | bytes 327680 | tf_op jit(solution)/shard_map/all_gather | solution.py:109
  569.4 0.8 convert_multiply_fusion.7
  570.3 0.8 convert_multiply_fusion.6
  571.1 57.5 %reduce-scatter.11.cloned.1.call-done = bf16[128,768]{1,0:T(8,128)(2,1)} async-done(((bf16[1024,768]{1,0:T(8,128)(2,1)}), bf16[128,768]{1,0:T(8,128)(2,1)}) %reduce-scatter.11.cloned.1.call-update) | async-done | bytes 196624 | tf_op jit(solution)/shard_map/reduce_scatter | solution.py:98
  628.6 10.4 %all_gather.44 = bf16[128,3072]{1,0:T(8,128)(2,1)S(1)} all-gather(bf16[128,768]{1,0:T(8,128)(2,1)} %reduce-scatter.11.cloned.1.call-done), channel_id=1, replica_groups=mesh['fsdp'=8,'rep'=4] {'rep'}, dimensions={1}, use_global_device_ids=true | all-gather | bytes 983040 | tf_op jit(solution)/shard_map/all_gather | solution.py:106
  639.1 1.3 convert_multiply_fusion.1
  640.4 56.1 %reduce-scatter.19.cloned.1.call-done = bf16[128,768]{1,0:T(8,128)(2,1)} async-done(((bf16[1024,768]{1,0:T(8,128)(2,1)}), bf16[128,768]{1,0:T(8,128)(2,1)}) %reduce-scatter.19.cloned.1.call-update) | async-done | bytes 196624 | tf_op jit(solution)/shard_map/reduce_scatter | solution.py:98
  696.5 10.4 %all_gather.46 = bf16[128,3072]{1,0:T(8,128)(2,1)S(1)} all-gather(bf16[128,768]{1,0:T(8,128)(2,1)} %reduce-scatter.19.cloned.1.call-done), channel_id=1, replica_groups=mesh['fsdp'=8,'rep'=4] {'rep'}, dimensions={1}, use_global_device_ids=true | all-gather | bytes 983040 | tf_op jit(solution)/shard_map/all_gather | solution.py:106
  706.9 1.3 convert_multiply_fusion
  (92 shorter events, 2.3 us)
Async XLA Ops:
  7.2 1.1 copy-start
  7.2 47.7 %all-gather.7.cloned.1.call-start = ((), (), s32[]{:S(2)}) async-start(), calls=%async_computation.8 | async-start | bytes 1769472 | tf_op jit(solution)/shard_map/all_gather | solution.py:79
  9.0 91.1 %all-gather.13.cloned.1.call-start = ((), (), s32[]{:S(2)}) async-start(), calls=%async_computation.11 | async-start | bytes 1769472 | tf_op jit(solution)/shard_map/all_gather | solution.py:79
  10.7 143.9 %all-gather.9.cloned.1.call-start = ((), (), s32[]{:S(2)}) async-start(), calls=%async_computation.9 | async-start | bytes 7864320 | tf_op jit(solution)/shard_map/all_gather | solution.py:83
  54.9 99.4 %copy-start.2 = (bf16[1,196,1024]{2,1,0:T(8,128)(2,1)S(1)}, bf16[1,196,1024]{2,1,0:T(8,128)(2,1)}, u32[]{:S(2)}) copy-start(bf16[1,196,1024]{2,1,0:T(8,128)(2,1)} %param.12) | copy-start | bytes 1204228
  54.9 99.4 %copy-start.13 = (bf16[1,8,1024]{2,1,0:T(8,128)(2,1)S(1)}, bf16[1,8,1024]{2,1,0:T(8,128)(2,1)}, u32[]{:S(2)}) copy-start(bf16[1,8,1024]{2,1,0:T(8,128)(2,1)} %param.14) | copy-start | bytes 49156
  54.9 140.1 %all-gather.15.cloned.1.call-start = ((), (), s32[]{:S(2)}) async-start(), calls=%async_computation.12 | async-start | bytes 7864320 | tf_op jit(solution)/shard_map/all_gather | solution.py:83
  100.2 54.3 %copy-start.15 = (bf16[1,8,1024]{2,1,0:T(8,128)(2,1)S(1)}, bf16[1,8,1024]{2,1,0:T(8,128)(2,1)}, u32[]{:S(2)}) copy-start(bf16[1,8,1024]{2,1,0:T(8,128)(2,1)} %param.23) | copy-start | bytes 49156
  100.2 54.4 %copy-start.12 = (bf16[1,196,1024]{2,1,0:T(8,128)(2,1)S(1)}, bf16[1,196,1024]{2,1,0:T(8,128)(2,1)}, u32[]{:S(2)}) copy-start(bf16[1,196,1024]{2,1,0:T(8,128)(2,1)} %param.21) | copy-start | bytes 1204228
  100.2 54.5 %copy-start.16 = (f32[1024]{0:T(1024)S(1)}, f32[1024]{0:T(1024)}, u32[]{:S(2)}) copy-start(f32[1024]{0:T(1024)} %param.15) | copy-start | bytes 12292
  100.2 119.1 %all-gather.11.cloned.1.call-start = ((), (), s32[]{:S(2)}) async-start(), calls=%async_computation.10 | async-start | bytes 2621440 | tf_op jit(solution)/shard_map/all_gather | solution.py:84
  126.6 120.3 %all-gather.17.cloned.1.call-start = ((), (), s32[]{:S(2)}) async-start(), calls=%async_computation.13 | async-start | bytes 2621440 | tf_op jit(solution)/shard_map/all_gather | solution.py:84
  154.3 122.4 %reduce-scatter.13.cloned.1.call-start = ((), (), s32[]{:S(2)}) async-start(), calls=%async_computation.16 | async-start | bytes 2621440 | tf_op jit(solution)/shard_map/reduce_scatter | solution.py:93
  160.0 3.5 copy-start.6
  160.2 3.3 copy-start.7
  166.0 2.2 copy-start.4
  166.1 2.3 copy-start.14
  168.1 26.9 %copy-start.17 = (f32[1024]{0:T(1024)S(1)}, f32[1024]{0:T(1024)}, u32[]{:S(2)}) copy-start(f32[1024]{0:T(1024)} %param.16) | copy-start | bytes 12292
  168.2 142.2 %reduce-scatter.21.cloned.1.call-start = ((), (), s32[]{:S(2)}) async-start(), calls=%async_computation.20 | async-start | bytes 2621440 | tf_op jit(solution)/shard_map/reduce_scatter | solution.py:93
  200.2 3.6 copy-start.10
  207.9 162.9 %reduce-scatter.9.cloned.1.call-start = ((), (), s32[]{:S(2)}) async-start(), calls=%async_computation.14 | async-start | bytes 7864320 | tf_op jit(solution)/shard_map/reduce_scatter | solution.py:90
  224.3 7.4 %copy-start.8 = (bf16[204,1024]{0,1:T(8,128)(2,1)S(1)}, bf16[204,1024]{0,1:T(8,128)(2,1)}, u32[]{:S(2)}) copy-start(bf16[204,1024]{0,1:T(8,128)(2,1)} %copy-done.7) | copy-start | bytes 1253380
  238.6 3.5 copy-start.3
  238.6 3.6 copy-start.18
  238.6 3.6 copy-start.20
  241.4 0.8 copy-start.23
  246.8 184.3 %reduce-scatter.17.cloned.1.call-start = ((), (), s32[]{:S(2)}) async-start(), calls=%async_computation.18 | async-start | bytes 7864320 | tf_op jit(solution)/shard_map/reduce_scatter | solution.py:90
  249.5 1.9 copy-start.9
  251.5 6.2 copy-start.11
  263.0 3.4 copy-start.5
  263.0 3.4 copy-start.21
  263.0 3.4 copy-start.24
  265.6 0.8 copy-start.25
  271.0 100.1 %copy-start.19 = (bf16[16,64,204]{2,1,0:T(8,128)(2,1)S(1)}, bf16[16,64,204]{2,1,0:T(8,128)(2,1)}, u32[]{:S(2)}) copy-start(bf16[16,64,204]{2,1,0:T(8,128)(2,1)} %fusion.40) | copy-start | bytes 1253380
  271.0 225.0 %reduce-scatter.15.cloned.1.call-start = ((), (), s32[]{:S(2)}) async-start(), calls=%async_computation.17 | async-start | bytes 589824 | tf_op jit(solution)/shard_map/reduce_scatter | solution.py:101
  276.7 284.1 %reduce-scatter.23.cloned.1.call-start = ((), (), s32[]{:S(2)}) async-start(), calls=%async_computation.21 | async-start | bytes 589824 | tf_op jit(solution)/shard_map/reduce_scatter | solution.py:101
  310.4 318.2 %reduce-scatter.11.cloned.1.call-start = ((), (), s32[]{:S(2)}) async-start(), calls=%async_computation.15 | async-start | bytes 1769472 | tf_op jit(solution)/shard_map/reduce_scatter | solution.py:98
  370.9 325.6 %reduce-scatter.19.cloned.1.call-start = ((), (), s32[]{:S(2)}) async-start(), calls=%async_computation.19 | async-start | bytes 1769472 | tf_op jit(solution)/shard_map/reduce_scatter | solution.py:98
  376.9 54.3 %copy-start.22 = (bf16[16,64,136]{2,1,0:T(8,128)(2,1)S(1)}, bf16[16,64,136]{2,1,0:T(8,128)(2,1)}, u32[]{:S(2)}) copy-start(bf16[16,64,136]{2,1,0:T(8,128)(2,1)} %fusion.34) | copy-start | bytes 835588
  639.1 69.1 %copy-start.1 = (bf16[128,3072]{1,0:T(8,128)(2,1)S(1)}, bf16[128,3072]{1,0:T(8,128)(2,1)}, u32[]{:S(2)}) copy-start(bf16[128,3072]{1,0:T(8,128)(2,1)} %param.17) | copy-start | bytes 2359300
Sparse Core Ops, SparseCore 0:
  10.8 44.0 all-gather.6
  57.6 42.5 all-gather.12
  101.7 45.4 all-gather.8
  148.6 46.3 all-gather.14
  196.4 22.8 all-gather.10
  220.7 22.8 all-gather.16
  246.1 30.5 reduce-scatter.12
  279.2 31.1 reduce-scatter.20
  312.9 57.8 reduce-scatter.8
  373.2 57.8 reduce-scatter.16
  434.5 61.4 reduce-scatter.14
  499.2 61.5 reduce-scatter.22
  564.2 64.3 reduce-scatter.10
  631.9 64.5 reduce-scatter.18
where the time goes:
time: 718 us; the launch traced here: 715 us
  waiting for transfers between devices  467 us (65%)
  blocking collectives  131 us (18%)
  matrix products  84.5 us (12%)
  between operations  14.3 us (2%)
  local copies, waits for them, and re-layouts  11 us (2%)
    reduce_scatter x2, waiting for transfers between devices, reduce_grads(): lax.psum_scatter(qkv_term.astype(jnp.bfloat16), 'rep', scatter_dimension=...  114 us
    reduce_scatter x2, waiting for transfers between devices, reduce_grads(): lax.psum_scatter(qkv_sum.astype(jnp.bfloat16), 'fsdp', scatter_dimension=...  114 us
    all_gather x2, waiting for transfers between devices, fetch(): lax.all_gather(qkv_part, 'fsdp', axis=0, tiled=True)  89.3 us
    reduce_scatter x2, waiting for transfers between devices, reduce_grads(): lax.psum_scatter(out_sum.astype(jnp.bfloat16), 'fsdp', scatter_dimension=...  72.9 us
    all_gather x2, blocking collectives, fetch(): lax.all_gather(out_part, 'fsdp', axis=0, tiled=True)  52.1 us
    psum x1, blocking collectives, per_device(): lax.psum((video_sums[2], audio_sums[2]), ('fsdp', 'rep'))  40.4 us
    reduce_scatter x2, waiting for transfers between devices, reduce_grads(): lax.psum_scatter(out_term.astype(jnp.bfloat16), 'rep', scatter_dimension=...  39.3 us
    all_gather x2, waiting for transfers between devices, fetch(): lax.all_gather(qkv_part, 'rep', axis=1, tiled=True)  26.6 us
  transfers between devices with their start and end apart: 14, of which 12 were waited for; matrix products, arithmetic and copies ran while one was open for 14% of the time, Pallas kernels for 0%

commit v1 on v0

v1 whole, which is shorter than its diff:
```python
import functools

import jax
import jax.numpy as jnp
from jax import lax
from jax.experimental import pallas as pl
from jax.experimental.pallas import tpu as pltpu
from jax.sharding import PartitionSpec as P

HEAD = 64
f32 = jnp.float32
bf16 = jnp.bfloat16


def remote(src, dst, send, recv, f, r):
    return pltpu.make_async_remote_copy(
        src_ref=src,
        dst_ref=dst,
        send_sem=send,
        recv_sem=recv,
        device_id={"fsdp": f, "rep": r},
        device_id_type=pl.DeviceIdType.MESH,
    )


def places(n, R):
    f = lax.axis_index("fsdp")
    r = lax.axis_index("rep")
    line = f // 2
    x = lax.rem(f, 2)
    return f, r, line, x, f + 1 - 2 * x


def greet(n, R):
    f, r, line, x, partner = places(n, R)
    barrier = pltpu.get_barrier_semaphore()

    def signal(ff, rr):
        pl.semaphore_signal(
            barrier,
            inc=1,
            device_id={"fsdp": ff, "rep": rr},
            device_id_type=pl.DeviceIdType.MESH,
        )

    signal(partner, r)
    for j in range(1, n // 2):
        signal(lax.rem(line + j, n // 2) * 2 + x, r)
    for j in range(1, R):
        signal(f, lax.rem(r + j, R))
    pl.semaphore_wait(barrier, n // 2 + R - 1)


def gather_kernel(n, R, oc, w_ref, tv_ref, ta_ref, wf, wo, gv, ga, zs, zr, xs, xr, ts, tr, os, orr, loc):
    L = n // 2
    G = n // R
    H = R // 2
    f, r, line, x, partner = places(n, R)
    mate = r + 1 - 2 * lax.rem(r, 2)
    greet(n, R)
    C = w_ref.shape[2]

    own = [pltpu.make_async_copy(w_ref.at[s], wf.at[s, f], loc.at[s]) for s in range(2)]
    own_t = [
        pltpu.make_async_copy(tv_ref, gv.at[r], loc.at[2]),
        pltpu.make_async_copy(ta_ref, ga.at[r], loc.at[3]),
    ]
    along = []
    across = []
    tokens = []
    relay = []
    for s in range(2):
        row = []
        for j in range(1, L):
            c = remote(w_ref.at[s], wf.at[s, f], zs.at[s, j], zr.at[s, j], lax.rem(line + j, L) * 2 + x, r)
            c.start()
            row.append(c)
        along.append(row)
        c = remote(w_ref.at[s], wf.at[s, f], xs.at[s, 0], xr.at[s, 0], partner, r)
        c.start()
        across.append([c])
        src, dst = (tv_ref, gv) if s == 0 else (ta_ref, ga)
        row = []
        for j in range(1, H):
            c = remote(src, dst.at[r], ts.at[s, j], tr.at[s, j], f, lax.rem(r + 2 * j, R))
            c.start()
            row.append(c)
        tokens.append(row)
        c = remote(src, dst.at[r], ts.at[s, 0], tr.at[s, 0], f, mate)
        c.start()
        relay.append([c])
    for c in own + own_t:
        c.start()
    for s in range(2):
        dst = gv if s == 0 else ga
        for j in range(1, L):
            along[s][j - 1].wait_recv()
            b = lax.rem(line - j + L, L) * 2 + x
            c = remote(wf.at[s, b], wf.at[s, b], xs.at[s, j], xr.at[s, j], partner, r)
            c.start()
            across[s].append(c)
        for j in range(1, H):
            tokens[s][j - 1].wait_recv()
            b = lax.rem(r - 2 * j + R, R)
            c = remote(dst.at[b], dst.at[b], ts.at[s, H - 1 + j], tr.at[s, H - 1 + j], f, mate)
            c.start()
            relay[s].append(c)
    swap = []
    for s in range(2):
        own[s].wait()
        for c in across[s]:
            c.wait_recv()
        for j in range(1, R):
            p = lax.rem(r + j, R)
            c = remote(
                wf.at[s, pl.ds(p * G, G), :, pl.ds(C - oc, oc)],
                wo.at[s, r],
                os.at[s, j],
                orr.at[s, j],
                f,
                p,
            )
            c.start()
            swap.append(c)
        c = pltpu.make_async_copy(
            wf.at[s, pl.ds(r * G, G), :, pl.ds(C - oc, oc)], wo.at[s, r], loc.at[4 + s]
        )
        c.start()
        own_t.append(c)
    for c in own_t:
        c.wait()
    for s in range(2):
        for c in along[s] + across[s] + tokens[s] + relay[s]:
            c.wait_send()
        for c in relay[s]:
            c.wait_recv()
    for c in swap:
        c.wait()


def gather(n, R, oc, w, tv, ta):
    _, rows, C = w.shape
    H = R // 2
    G = n // R
    dma = pltpu.SemaphoreType.DMA
    vm = pl.BlockSpec(memory_space=pltpu.VMEM)
    return pl.pallas_call(
        functools.partial(gather_kernel, n, R, oc),
        out_shape=(
            jax.ShapeDtypeStruct((2, n, rows, C), bf16),
            jax.ShapeDtypeStruct((2, R, G, rows, oc), bf16),
            jax.ShapeDtypeStruct((R,) + tv.shape, bf16),
            jax.ShapeDtypeStruct((R,) + ta.shape, bf16),
        ),
        in_specs=[vm] * 3,
        out_specs=(vm,) * 4,
        scratch_shapes=[
            dma((2, n // 2)),
            dma((2, n // 2)),
            dma((2, n // 2)),
            dma((2, n // 2)),
            dma((2, 2 * H)),
            dma((2, 2 * H)),
            dma((2, R)),
            dma((2, R)),
            dma((6,)),
        ],
        compiler_params=pltpu.CompilerParams(
            collective_id=0, has_side_effects=True, vmem_limit_bytes=60 * 1024 * 1024
        ),
    )(w, tv, ta)


def reduce_kernel(n, R, oc, gq, go, dv, da, gain, fin, rv, ra, gsum,
                  ob, xq, xo, sq, so, zq, zo, fb, gx, gb, gc,
                  as_, ar, qs, qr, ps, pr, us, ur, vs, vr, es, er, ds_, dr, ks, kr, loc):
    L = n // 2
    G = n // R
    f, r, line, x, partner = places(n, R)
    C3 = gq.shape[3]
    greet(n, R)
    done = []
    turn = []
    own = []
    for s in range(2):
        row = []
        for j in range(1, R):
            p = lax.rem(r + j, R)
            c = remote(
                go.at[s, :, :, pl.ds(pl.multiple_of(p * oc, oc), oc)],
                ob.at[s, pl.ds(r * G, G)],
                as_.at[s, j],
                ar.at[s, j],
                f,
                p,
            )
            c.start()
            row.append(c)
        turn.append(row)
        c = pltpu.make_async_copy(
            go.at[s, :, :, pl.ds(pl.multiple_of(r * oc, oc), oc)],
            ob.at[s, pl.ds(r * G, G)],
            loc.at[s],
        )
        c.start()
        own.append(c)
    cg = remote(gain, gx, ks.at[0], kr.at[0], partner, r)
    cg.start()
    cross_q = []
    for s in range(2):
        row = []
        for k in range(L):
            j = lax.rem(line + k, L)
            c = remote(gq.at[s, 2 * j + 1 - x], xq.at[s, j], qs.at[s, k], qr.at[s, k], partner, r)
            c.start()
            row.append(c)
        cross_q.append(row)
    back = []
    for s, (src, dst) in enumerate(((dv, rv), (da, ra))):
        for j in range(1, R):
            p = lax.rem(r + j, R)
            c = remote(src.at[p], dst.at[j - 1], ds_.at[s, j], dr.at[s, j], f, p)
            c.start()
            back.append(c)
    cg.wait_recv()
    gb[line] = gain[...] + gx[...]
    line_g = []
    for j in range(1, L):
        c = remote(gb.at[line], gb.at[line], ks.at[j], kr.at[j], lax.rem(line + j, L) * 2 + x, r)
        c.start()
        line_g.append(c)
    cross_o = []
    for s in range(2):
        own[s].wait()
        for c in turn[s]:
            c.wait_recv()
        row = []
        for k in range(L):
            j = lax.rem(line + k, L)
            c = remote(ob.at[s, 2 * j + 1 - x], xo.at[s, j], ps.at[s, k], pr.at[s, k], partner, r)
            c.start()
            row.append(c)
        cross_o.append(row)
    for c in line_g:
        c.wait_recv()
    total = gb[0]
    for j in range(1, L):
        total = total + gb[j]
    gc[r] = total
    group_g = []
    for j in range(1, R):
        c = remote(gc.at[r], gc.at[r], ks.at[L + j], kr.at[L + j], f, lax.rem(r + j, R))
        c.start()
        group_g.append(c)
    along_q = []
    along_o = []
    for s in range(2):
        row_q = []
        row_o = []
        for k in list(range(1, L)) + [0]:
            j = lax.rem(line + k, L)
            cross_q[s][k].wait_recv()
            sq[s, j] = (gq[s, 2 * j + x].astype(f32) + xq[s, j].astype(f32)).astype(bf16)
            if k:
                c = remote(sq.at[s, j], zq.at[s, k - 1], us.at[s, k], ur.at[s, k], 2 * j + x, r)
                c.start()
                row_q.append(c)
            cross_o[s][k].wait_recv()
            so[s, j] = (ob[s, 2 * j + x].astype(f32) + xo[s, j].astype(f32)).astype(bf16)
            if k:
                c = remote(so.at[s, j], zo.at[s, k - 1], vs.at[s, k], vr.at[s, k], 2 * j + x, r)
                c.start()
                row_o.append(c)
        along_q.append(row_q)
        along_o.append(row_o)
    spread = []
    for s in range(2):
        tq = sq[s, line].astype(f32)
        to = so[s, line].astype(f32)
        for k in range(1, L):
            along_q[s][k - 1].wait_recv()
            tq = tq + zq[s, k - 1].astype(f32)
            along_o[s][k - 1].wait_recv()
            to = to + zo[s, k - 1].astype(f32)
        fb[s, :, pl.ds(0, C3)] = tq.astype(bf16)
        fb[s, :, pl.ds(C3, oc)] = to.astype(bf16)
        fin[s, r, :, pl.ds(0, C3)] = tq.astype(bf16)
        fin[s, r, :, pl.ds(C3, oc)] = to.astype(bf16)
        for j in range(1, R):
            c = remote(fb.at[s], fin.at[s, r], es.at[s, j], er.at[s, j], f, lax.rem(r + j, R))
            c.start()
            spread.append(c)
    for c in group_g:
        c.wait_recv()
    total = gc[0]
    for j in range(1, R):
        total = total + gc[j]
    gsum[...] = total
    for c in back + spread:
        c.wait()
    for c in [cg] + line_g + group_g:
        c.wait_send()
    for s in range(2):
        for c in turn[s] + cross_q[s] + cross_o[s] + along_q[s] + along_o[s]:
            c.wait_send()


def reduce_all(n, R, oc, gq, go, dv, da, gain):
    _, _, rows, C3 = gq.shape
    L = n // 2
    C = C3 + oc
    dma = pltpu.SemaphoreType.DMA
    vm = pl.BlockSpec(memory_space=pltpu.VMEM)
    V = pltpu.VMEM
    return pl.pallas_call(
        functools.partial(reduce_kernel, n, R, oc),
        out_shape=(
            jax.ShapeDtypeStruct((2, R, rows, C), bf16),
            jax.ShapeDtypeStruct((R - 1,) + dv.shape[1:], bf16),
            jax.ShapeDtypeStruct((R - 1,) + da.shape[1:], bf16),
            jax.ShapeDtypeStruct(gain.shape, f32),
        ),
        in_specs=[vm] * 5,
        out_specs=(vm,) * 4,
        scratch_shapes=[
            V((2, n, rows, oc), bf16),
            V((2, L, rows, C3), bf16),
            V((2, L, rows, oc), bf16),
            V((2, L, rows, C3), bf16),
            V((2, L, rows, oc), bf16),
            V((2, L - 1, rows, C3), bf16),
            V((2, L - 1, rows, oc), bf16),
            V((2, rows, C), bf16),
            V(gain.shape, f32),
            V((L,) + gain.shape, f32),
            V((R,) + gain.shape, f32),
            dma((2, R)),
            dma((2, R)),
            dma((2, L)),
            dma((2, L)),
            dma((2, L)),
            dma((2, L)),
            dma((2, L)),
            dma((2, L)),
            dma((2, L)),
            dma((2, L)),
            dma((2, R)),
            dma((2, R)),
            dma((2, R)),
            dma((2, R)),
            dma((L + R,)),
            dma((L + R,)),
            dma((2,)),
        ],
        compiler_params=pltpu.CompilerParams(
            collective_id=1, has_side_effects=True, vmem_limit_bytes=60 * 1024 * 1024
        ),
    )(gq, go, dv, da, gain)


def normalise(z):
    zf = z.astype(f32)
    inverse = lax.rsqrt(jnp.mean(zf * zf, axis=-1, keepdims=True) + 1e-06)
    return zf * inverse, inverse


def stream(z, dyb, gain, w, wo, length):
    clips, rows, width = z.shape
    cols = w.shape[1] // 3
    normed, _ = normalise(z)
    hidden = (normed * gain).astype(bf16)
    qkv = jnp.einsum("csd,de->cse", hidden, w, preferred_element_type=f32).astype(bf16)
    scale = HEAD ** (-0.5)
    query = qkv[..., :cols].reshape(clips, rows, -1, HEAD)
    keyed = qkv[..., cols : 2 * cols].reshape(clips, rows, -1, HEAD)
    valued = qkv[..., 2 * cols :].reshape(clips, rows, -1, HEAD)
    scores = jnp.einsum("cshd,cthd->chst", query, keyed, preferred_element_type=f32) * scale
    real = lax.broadcasted_iota(jnp.int32, scores.shape, 3) < length
    probs = jax.nn.softmax(jnp.where(real, scores, -1e30), axis=-1)
    pb = probs.astype(bf16)
    att = (
        jnp.einsum("chst,cthd->cshd", pb, valued, preferred_element_type=f32)
        .reshape(clips, rows, cols)
        .astype(bf16)
    )
    out_term = jnp.einsum("csd,cse->de", att, dyb, preferred_element_type=f32).astype(bf16)
    datt = jnp.einsum("cse,de->csd", dyb, wo, preferred_element_type=f32).astype(bf16)
    datt = datt.reshape(clips, rows, -1, HEAD)
    dprob = jnp.einsum("cshd,cthd->chst", datt, valued, preferred_element_type=f32)
    dvalue = jnp.einsum("chst,cshd->cthd", pb, datt, preferred_element_type=f32)
    dscore = probs * (dprob - jnp.sum(probs * dprob, axis=-1, keepdims=True)) * scale
    dsb = dscore.astype(bf16)
    dquery = jnp.einsum("chst,cthd->cshd", dsb, keyed, preferred_element_type=f32)
    dkey = jnp.einsum("chst,cshd->cthd", dsb, query, preferred_element_type=f32)
    dqkv = jnp.concatenate(
        [t.astype(bf16).reshape(clips, rows, cols) for t in (dquery, dkey, dvalue)], 2
    )
    qkv_term = jnp.einsum("csd,cse->de", hidden, dqkv, preferred_element_type=f32).astype(bf16)
    dhidden = jnp.einsum("cse,de->csd", dqkv, w, preferred_element_type=f32)
    gain_term = jnp.sum(dhidden * normed, axis=(0, 1))
    return qkv_term, out_term, dhidden.astype(bf16), gain_term


def d_rows(z, d_out, dh, gain):
    normed, inverse = normalise(z)
    dnorm = dh * gain
    return d_out + inverse * (dnorm - normed * jnp.mean(dnorm * normed, axis=-1, keepdims=True))


def padded(tokens, bottle):
    rows = tokens.shape[1] + bottle.shape[1]
    return jnp.pad(jnp.concatenate([tokens, bottle], 1), ((0, 0), (0, -rows % 16), (0, 0)))


def per_device(
    n,
    R,
    video_in,
    audio_in,
    bottle_in,
    video_gain,
    audio_gain,
    video_qkv,
    video_out,
    audio_qkv,
    audio_out,
    grad_video,
    grad_audio,
    grad_bottle,
):
    r = lax.axis_index("rep")
    clips = video_in.shape[0]
    count = float(clips * n * R)
    rows, width = video_out.shape
    oc = width // R

    def quarter(qkv, out):
        parts = [lax.dynamic_slice_in_dim(qkv, k * width + r * oc, oc, 1) for k in range(3)]
        return jnp.concatenate(parts + [lax.dynamic_slice_in_dim(out, r * oc, oc, 1)], 1)

    w = jnp.stack([quarter(video_qkv, video_out), quarter(audio_qkv, audio_out)])
    half = (grad_bottle.astype(f32) * 0.5).astype(bf16)
    zs = [padded(video_in, bottle_in), padded(audio_in, bottle_in)]
    dys = [padded(grad_video, half), padded(grad_audio, half)]
    tv, ta = [jnp.stack([z, dy]) for z, dy in zip(zs, dys)]
    wf, wo, gv, ga = gather(n, R, oc, w, tv, ta)

    lengths = [t.shape[1] + bottle_in.shape[1] for t in (video_in, audio_in)]
    gains = [video_gain, audio_gain]
    results = []
    for s, got in enumerate((gv, ga)):
        full = wf[s].reshape(n * rows, -1)[:, : 3 * oc]
        rows_out = jnp.moveaxis(wo[s].reshape(R, oc, oc), 0, 1).reshape(oc, width)
        p = got.shape[3]
        z = got[:, 0].reshape(R * clips, p, width)
        dy = got[:, 1].reshape(R * clips, p, width)
        results.append(stream(z, dy, gains[s], full, rows_out, lengths[s]))
    gq = jnp.stack([res[0].reshape(n, rows, 3 * oc) for res in results])
    go = jnp.stack([res[1].reshape(n // R, rows, width) for res in results])
    dhs = [res[2].reshape((R, clips) + res[2].shape[1:]) for res in results]
    gain_terms = jnp.stack([res[3] for res in results])
    fin, rv, ra, gsum = reduce_all(n, R, oc, gq, go, dhs[0], dhs[1], gain_terms)
    gsum = gsum / count

    dzs = []
    for s, got in enumerate((rv, ra)):
        dh = lax.dynamic_index_in_dim(dhs[s], r, 0, keepdims=False).astype(f32)
        for j in range(R - 1):
            dh = dh + got[j].astype(f32)
        dzs.append(d_rows(zs[s], dys[s].astype(f32), dh, gains[s]))
    grads = []
    for s in range(2):
        q = jnp.moveaxis(fin[s, :, :, : 3 * oc].reshape(R, rows, 3, oc), 0, 2)
        grads.append(q.reshape(rows, 3 * width).astype(f32) / count)
        o = jnp.moveaxis(fin[s, :, :, 3 * oc :], 0, 1)
        grads.append(o.reshape(rows, width).astype(f32) / count)
    tv_len, ta_len = video_in.shape[1], audio_in.shape[1]
    dbottle = dzs[0][:, tv_len : lengths[0]] + dzs[1][:, ta_len : lengths[1]]
    return (
        dzs[0][:, :tv_len].astype(bf16),
        dzs[1][:, :ta_len].astype(bf16),
        dbottle.astype(bf16),
        grads[0],
        grads[1],
        grads[2],
        grads[3],
        gsum[0],
        gsum[1],
    )


def solution(mesh):
    n = mesh.shape["fsdp"]
    R = mesh.shape["rep"]
    clip = P(("fsdp", "rep"), None, None)
    shard = P("fsdp", None)
    in_specs = (clip, clip, clip, P(), P(), shard, shard, shard, shard, clip, clip, clip)
    out_specs = (clip, clip, clip, shard, shard, shard, shard, P(), P())
    return jax.shard_map(
        functools.partial(per_device, n, R),
        mesh=mesh,
        in_specs=in_specs,
        out_specs=out_specs,
        check_vma=False,
    )
```

time: 718 us -> 307 us (0.43)
  waiting for transfers between devices: 467 us -> 0 us
  Pallas kernels: 0 us -> 175 us
  blocking collectives: 131 us -> 0 us
  local copies, waits for them, and re-layouts: 11 us -> 38.3 us
  other arithmetic: 6.5 us -> 21.9 us
  matrix products: 84.5 us -> 69.9 us
  between operations: 14.3 us -> 1.3 us
    reduce_scatter x8 -> x0, waiting for transfers between devices: 340 us -> none  [the longest x2 114 us: reduce_grads(): lax.psum_scatter(qkv_term.astype(jnp.bfloat16), 'rep', scatter_dimension=...]
    pallas_call x0 -> x2, Pallas kernels: none -> 175 us  [the longest x1 102 us: reduce_all(): pl.pallas_call(functools.partial(reduce_kernel, n, R, oc), out_shape=(jax...]
    all_gather x6 -> x0, waiting for transfers between devices: 127 us -> none  [the longest x2 89.3 us: fetch(): lax.all_gather(qkv_part, 'fsdp', axis=0, tiled=True)]
    all_gather x6 -> x0, blocking collectives: 90.2 us -> none  [the longest x2 52.1 us: fetch(): lax.all_gather(out_part, 'fsdp', axis=0, tiled=True)]
    psum x1 -> x0, blocking collectives: 40.4 us -> none  [per_device(): lax.psum((video_sums[2], audio_sums[2]), ('fsdp', 'rep'))]
    dot_general x20, matrix products: 78 us -> 62.3 us  [the longest x2 11.1 us: stream(): jnp.einsum('chst,cthd->cshd', dsb, keyed, preferred_element_type=f32)]
    reshape x4 -> x12, local copies, waits for them, and re-layouts: 1.61 us -> 15.5 us  [the longest x6 9.83 us: stream(): t.astype(bf16).reshape(clips, rows, cols)]
    slice x7 -> x10, local copies, waits for them, and re-layouts: 2.31 us -> 9.64 us  [the longest x1 4.21 us: per_device(): full = wf[s].reshape(n * rows, -1)[:, :3 * oc]]
  transfers between devices with their start and end apart: 14 -> 0, of which waited for: 12 -> 0; matrix products, arithmetic and copies ran while one was open for 14% -> 0% of each run, Pallas kernels for 0% -> 0%
where the time goes in v1:
time: 307 us
  Pallas kernels  175 us (57%)
  matrix products  69.9 us (23%)
  local copies, waits for them, and re-layouts  38.3 us (12%)
  other arithmetic  21.9 us (7%)
    pallas_call x1, Pallas kernels, reduce_all(): pl.pallas_call(functools.partial(reduce_kernel, n, R, oc), out_shape=(jax...  102 us
    pallas_call x1, Pallas kernels, gather(): pl.pallas_call(functools.partial(gather_kernel, n, R, oc), out_shape=(jax...  73.6 us
    dot_general x2, matrix products, stream(): jnp.einsum('chst,cthd->cshd', dsb, keyed, preferred_element_type=f32)  11.1 us
    dot_general x2, matrix products, stream(): dkey = jnp.einsum('chst,cshd->cthd', dsb, query, preferred_element_type=f32)  10.4 us
    reshape x6, local copies, waits for them, and re-layouts, stream(): t.astype(bf16).reshape(clips, rows, cols)  9.83 us
    dot_general x2, matrix products, stream(): dhidden = jnp.einsum('cse,de->csd', dqkv, w, preferred_element_type=f32)  9.16 us
    sub x2, matrix products, stream(): probs = jax.nn.softmax(jnp.where(real, scores, -1e+30), axis=-1)  7.51 us
    unnamed x102, local copies, waits for them, and re-layouts  6.27 us

profile of v1, /device:TPU:13, one launch (start us, length us, event | category | flops | bytes accessed | tf_op | source)
XLA Modules:
  0.0 306.6 jit_solution(1822969965283887105)
XLA Ops:
  1.8 1.2 fusion.86
  3.6 1.1 fusion.102
  5.3 0.7 multiply_convert_fusion.2
  6.0 0.9 constant_dynamic-slice_fusion
  6.9 1.0 constant_dynamic-slice_fusion.3
  8.0 0.8 pad_maximum_fusion.6.w_ref
  8.9 0.9 pad_maximum_fusion.5.ta_ref
  9.9 1.0 pad_maximum_fusion.4.tv_ref
  10.9 73.6 %shard_map.187 = (bf16[2,8,128,1024]{3,2,1,0:T(8,128)(2,1)}, bf16[2,4,2,128,256]{4,3,2,1,0:T(8,128)(2,1)}, bf16[4,2,1,208,1024]{4,3,2,1,0:T(8,128)(2,1)}, bf16[4,2,1,144,1024]{4,3,2,1,0:T(8,128)(2,1)}) custom-call(bf16[2,128,1024]{2,1,0:T(8,128)(2,1)} %pad_maximum_fusion.6.w_ref, bf16[2,1,208,1024]{3,2,1,0:T(8,128)(2,1)} %pad_maximum_fusion.4.tv_ref, ...), custom_call_target="tpu_custom_call" | custom-call | tf_op jit(solution)/shard_map/pallas_call | solution.py:147
  84.5 4.2 %fusion.139 = (bf16[1,8,128,1024]{3,2,1,0:T(8,128)(2,1)}, bf16[1,8,128,1024]{3,2,1,0:T(8,128)(2,1)S(1)}) fusion(bf16[2,8,128,1024]{3,2,1,0:T(8,128)(2,1)} %get-tuple-element.18), kind=kLoop, calls=%fused_computation.180 | loop fusion | bytes 8388608 | tf_op jit(solution)/shard_map/slice | solution.py:452
  89.1 0.9 add_rsqrt_fusion.1
  90.4 1.1 convolution_convert_fusion.1
  91.6 1.0 copy.149
  92.6 1.0 copy.147
  93.6 1.0 copy.146
  95.5 2.9 fusion.64
  99.1 2.6 convolution_convert_fusion.6
  101.8 1.2 copy.98
  103.0 2.0 copy.148
  105.0 3.0 convolution_convert_fusion
  108.1 1.0 copy.99
  109.1 1.0 copy.96
  110.1 1.0 copy.95
  111.1 1.7 fusion.147
  112.9 4.3 %fusion.145 = (f32[4,4,144]{2,1,0:T(4,128)}, f32[4,4,144,144]{2,3,1,0:T(8,128)}) fusion(pred[144]{0:T(512)(128)(4,1)} %iota_compare_fusion.2, bf16[4,144,4,64]{1,3,2,0:T(8,128)(2,1)} %bitcast.228, bf16[4,144,4,64]{1,3,2,0:T(8,128)(2,1)} %bitcast.230), kind=kOutput, calls=%fused_computation.186 | convolution fusion | flops 43794576 | bytes 1926288 | tf_op jit(solution)/shard_map/sub | solution.py:379
  117.2 3.1 %convolution_convert_fusion.4 = bf16[4,4,64,144]{3,2,1,0:T(8,128)(2,1)} fusion(bf16[4,144,4,64]{1,3,2,0:T(8,128)(2,1)} %bitcast.215, f32[4,4,144,144]{2,3,1,0:T(8,128)} %get-tuple-element.72, f32[4,4,144]{2,1,0:T(4,128)} %get-tuple-element.71), kind=kOutput, calls=%fused_computation.65 | convolution fusion | flops 43278336 | bytes 1926144 | tf_op jit(solution)/shard_map/chst,cshd->cthd/dot_general | solution.py:390
  120.2 2.0 copy.119
  122.2 4.3 %fusion.55 = bf16[4,4,64,144]{3,2,1,0:T(8,128)(2,1)} fusion(bf16[4,144,4,64]{1,3,2,0:T(8,128)(2,1)} %bitcast.229, f32[4,4,144,144]{2,3,1,0:T(8,128)S(1)} %fusion.147, f32[4,4,144,144]{2,3,1,0:T(8,128)} %get-tuple-element.72, f32[4,4,144]{2,1,0:T(4,128)} %get-tuple-element.71), kind=kOutput, calls=%fused_computation.60 | convolution fusion | flops 44939664 | bytes 3253248 | tf_op jit(solution)/shard_map/chst,cshd->cthd/dot_general | solution.py:394
  126.5 4.2 %fusion.52 = bf16[4,4,64,144]{3,2,1,0:T(8,128)(2,1)} fusion(bf16[4,144,4,64]{1,3,2,0:T(8,128)(2,1)} %bitcast.231, f32[4,4,144,144]{2,3,1,0:T(8,128)S(1)} %fusion.147, f32[4,4,144,144]{2,3,1,0:T(8,128)} %get-tuple-element.72, f32[4,4,144]{2,1,0:T(4,128)} %get-tuple-element.71), kind=kOutput, calls=%fused_computation.59 | convolution fusion | flops 44939664 | bytes 3253248 | tf_op jit(solution)/shard_map/chst,cthd->cshd/dot_general | solution.py:393
  130.7 2.2 convolution_convert_fusion.2
  133.3 1.6 fusion.48
  134.9 2.0 copy.117
  136.8 2.0 copy.118
  138.8 4.4 %fusion.16 = (f32[1024]{0:T(1024)}, bf16[4,144,1024]{2,1,0:T(8,128)(2,1)}) fusion(f32[4,144]{1,0:T(4,128)S(1)} %copy-done.44, bf16[4,2,1,144,1024]{4,3,2,1,0:T(8,128)(2,1)} %get-tuple-element.20, bf16[1024,1024]{1,0:T(8,128)(2,1)S(1)} %bitcast.221, bf16[4,144,256]{2,1,0:T(8,128)(2,1)} %copy.119, bf16[4,144,256]{2,1,0:T(8,128)(2,1)} %copy.118, ...), kind=kOutput, calls=%fused_computation.25 | convolution fusion | flops 911571968 | bytes 4825088 | tf_op jit(solution)/shard_map/cse,de->csd/dot_general | solution.py:399
  143.3 2.7 bitcast_convert_fusion
  146.0 2.4 fusion.146
  148.5 3.2 %fusion.144 = (f32[4,4,208]{2,1,0:T(4,128)S(1)}, f32[4,4,208,208]{2,3,1,0:T(8,128)}) fusion(pred[208]{0:T(512)(128)(4,1)S(1)} %copy-done.46, bf16[4,208,4,64]{1,3,2,0:T(8,128)(2,1)S(1)} %bitcast.224, bf16[4,208,4,64]{1,3,2,0:T(8,128)(2,1)S(1)} %bitcast.226), kind=kOutput, calls=%fused_computation.185 | convolution fusion | flops 91373776 | bytes 3634384 | tf_op jit(solution)/shard_map/sub | solution.py:379
  151.7 2.6 convolution_convert_fusion.5
  154.3 1.0 copy.105
  155.3 6.1 %fusion.61 = bf16[4,4,64,208]{3,2,1,0:T(8,128)(2,1)S(1)} fusion(bf16[4,208,4,64]{1,3,2,0:T(8,128)(2,1)S(1)} %bitcast.225, f32[4,4,208,208]{2,3,1,0:T(8,128)} %fusion.146, f32[4,4,208,208]{2,3,1,0:T(8,128)} %get-tuple-element.70, f32[4,4,208]{2,1,0:T(4,128)} %copy-done.47), kind=kOutput, calls=%fused_computation.62 | convolution fusion | flops 93666768 | bytes 6403072 | tf_op jit(solution)/shard_map/chst,cshd->cthd/dot_general | solution.py:394
  161.4 6.8 %fusion.58 = bf16[4,4,64,208]{3,2,1,0:T(8,128)(2,1)} fusion(bf16[4,208,4,64]{1,3,2,0:T(8,128)(2,1)S(1)} %bitcast.227, f32[4,4,208,208]{2,3,1,0:T(8,128)} %fusion.146, f32[4,4,208,208]{2,3,1,0:T(8,128)} %get-tuple-element.70, f32[4,4,208]{2,1,0:T(4,128)S(1)} %copy-done.48), kind=kOutput, calls=%fused_computation.61 | convolution fusion | flops 93666768 | bytes 6403072 | tf_op jit(solution)/shard_map/chst,cthd->cshd/dot_general | solution.py:393
  168.3 2.5 convolution_convert_fusion.3
  171.3 0.7 fusion.49
  172.1 1.1 pad_maximum_fusion.2.go
  173.1 2.0 copy.103
  175.2 1.0 copy.104
  176.2 4.7 %fusion.7 = (f32[1024]{0:T(1024)S(1)}, bf16[4,208,1024]{2,1,0:T(8,128)(2,1)}) fusion(f32[4,208]{1,0:T(4,128)S(1)} %copy-done.42, bf16[4,2,1,208,1024]{4,3,2,1,0:T(8,128)(2,1)} %get-tuple-element.17, bf16[1024,1024]{1,0:T(8,128)(2,1)S(1)} %bitcast.219, bf16[4,208,256]{2,1,0:T(8,128)(2,1)} %copy.105, bf16[4,208,256]{2,1,0:T(8,128)(2,1)} %copy.104, ...), kind=kOutput, calls=%fused_computation.9 | convolution fusion | flops 1316715520 | bytes 6266880 | tf_op jit(solution)/shard_map/cse,de->csd/dot_general | solution.py:399
  181.0 2.3 bitcast_convert_fusion.1
  183.3 0.6 pad_maximum_fusion.11.gain
  183.9 2.0 pad_maximum_fusion.gq
  186.0 101.6 %shard_map.188 = (bf16[2,4,128,1024]{3,2,1,0:T(8,128)(2,1)}, bf16[3,1,208,1024]{3,2,1,0:T(8,128)(2,1)}, bf16[3,1,144,1024]{3,2,1,0:T(8,128)(2,1)}, f32[2,1024]{1,0:T(2,128)}) custom-call(bf16[2,8,128,768]{3,2,1,0:T(8,128)(2,1)} %pad_maximum_fusion.gq, bf16[2,2,128,1024]{3,2,1,0:T(8,128)(2,1)} %pad_maximum_fusion.2.go, bf16[4,1,208,1024]{3,2,1,0:T(8,128)(2,1)} %bitcast.204, ...), custom_call_target="tpu_custom_call" | custom-call | tf_op jit(solution)/shard_map/pallas_call | solution.py:315
  287.6 0.8 broadcast_multiply_fusion
  288.5 0.6 fusion.143
  289.1 1.8 fusion.82
  292.3 0.6 fusion.120
  292.9 0.8 slice.222
  293.7 0.7 slice.223
  294.4 1.1 multiply_bitcast_fusion
  295.8 1.0 copy.135
  297.0 1.0 copy.133
  298.0 2.8 convert_multiply_fusion.4
  301.4 1.6 copy.134
  303.0 1.9 copy.126
  305.0 1.6 copy.132
  (126 shorter events, 8.2 us)
Async XLA Ops:
  0.6 8.2 %copy-start.14 = (bf16[1,8,1024]{2,1,0:T(8,128)(2,1)S(1)}, bf16[1,8,1024]{2,1,0:T(8,128)(2,1)}, u32[]{:S(2)}) copy-start(bf16[1,8,1024]{2,1,0:T(8,128)(2,1)} %param.14) | copy-start | bytes 49156
  0.7 8.2 %copy-start.2 = (bf16[1,128,1024]{2,1,0:T(8,128)(2,1)S(1)}, bf16[1,128,1024]{2,1,0:T(8,128)(2,1)}, u32[]{:S(2)}) copy-start(bf16[1,128,1024]{2,1,0:T(8,128)(2,1)} %param.13) | copy-start | bytes 786436
  0.7 8.2 %copy-start.17 = (bf16[1,128,1024]{2,1,0:T(8,128)(2,1)S(1)}, bf16[1,128,1024]{2,1,0:T(8,128)(2,1)}, u32[]{:S(2)}) copy-start(bf16[1,128,1024]{2,1,0:T(8,128)(2,1)} %param.22) | copy-start | bytes 786436
  6.0 3.8 %copy-start.31 = (bf16[1,8,1024]{2,1,0:T(8,128)(2,1)}, bf16[1,8,1024]{2,1,0:T(8,128)(2,1)S(1)}, u32[]{:S(2)}) copy-start(bf16[1,8,1024]{2,1,0:T(8,128)(2,1)S(1)} %multiply_convert_fusion.2) | copy-start | bytes 49156
  8.0 1.8 copy-start
  8.0 1.8 copy-start.11
  84.5 4.2 %copy-start.19 = (bf16[4,2,1,208,1024]{4,3,2,1,0:T(8,128)(2,1)S(1)}, bf16[4,2,1,208,1024]{4,3,2,1,0:T(8,128)(2,1)}, u32[]{:S(2)}) copy-start(bf16[4,2,1,208,1024]{4,3,2,1,0:T(8,128)(2,1)} %get-tuple-element.17) | copy-start | bytes 10223620
  84.5 5.5 %copy-start.22 = (bf16[4,2,1,144,1024]{4,3,2,1,0:T(8,128)(2,1)S(1)}, bf16[4,2,1,144,1024]{4,3,2,1,0:T(8,128)(2,1)}, u32[]{:S(2)}) copy-start(bf16[4,2,1,144,1024]{4,3,2,1,0:T(8,128)(2,1)} %get-tuple-element.20) | copy-start | bytes 7077892
  88.7 2.8 copy-start.9
  88.7 1.6 copy-start.37
  90.3 1.2 copy-start.43
  91.5 3.1 %copy-start.16 = (bf16[2,4,2,128,256]{4,3,2,1,0:T(8,128)(2,1)S(1)}, bf16[2,4,2,128,256]{4,3,2,1,0:T(8,128)(2,1)}, u32[]{:S(2)}) copy-start(bf16[2,4,2,128,256]{4,3,2,1,0:T(8,128)(2,1)} %get-tuple-element.19) | copy-start | bytes 3145732
  99.1 5.8 %copy-start.7 = (bf16[1,8,128,1024]{3,2,1,0:T(8,128)(2,1)S(1)}, bf16[1,8,128,1024]{3,2,1,0:T(8,128)(2,1)}, u32[]{:S(2)}) copy-start(bf16[1,8,128,1024]{3,2,1,0:T(8,128)(2,1)} %get-tuple-element.43) | copy-start | bytes 6291460
  130.7 2.5 copy-start.23
  133.3 5.5 %copy-start.10 = (bf16[1,8,128,1024]{3,2,1,0:T(8,128)(2,1)S(1)}, bf16[1,8,128,1024]{3,2,1,0:T(8,128)(2,1)}, u32[]{:S(2)}) copy-start(bf16[1,8,128,1024]{3,2,1,0:T(8,128)(2,1)} %copy-done.9) | copy-start | bytes 6291460
  133.3 5.5 %copy-start.44 = (f32[4,144]{1,0:T(4,128)S(1)}, f32[4,144]{1,0:T(4,128)}, u32[]{:S(2)}) copy-start(f32[4,144]{1,0:T(4,128)} %copy-done.43) | copy-start | bytes 6916
  138.8 4.5 %copy-start.24 = (bf16[4,2,1,144,1024]{4,3,2,1,0:T(8,128)(2,1)S(1)}, bf16[4,2,1,144,1024]{4,3,2,1,0:T(8,128)(2,1)}, u32[]{:S(2)}) copy-start(bf16[4,2,1,144,1024]{4,3,2,1,0:T(8,128)(2,1)} %get-tuple-element.20) | copy-start | bytes 7077892
  138.8 4.5 %copy-start.33 = (bf16[4,144,256]{2,1,0:T(8,128)(2,1)S(1)}, bf16[4,144,256]{2,1,0:T(8,128)(2,1)}, u32[]{:S(2)}) copy-start(bf16[4,144,256]{2,1,0:T(8,128)(2,1)} %copy.119) | copy-start | bytes 884740
  138.8 4.5 %copy-start.34 = (bf16[4,144,256]{2,1,0:T(8,128)(2,1)S(1)}, bf16[4,144,256]{2,1,0:T(8,128)(2,1)}, u32[]{:S(2)}) copy-start(bf16[4,144,256]{2,1,0:T(8,128)(2,1)} %copy.117) | copy-start | bytes 884740
  138.8 4.5 %copy-start.35 = (bf16[4,144,256]{2,1,0:T(8,128)(2,1)S(1)}, bf16[4,144,256]{2,1,0:T(8,128)(2,1)}, u32[]{:S(2)}) copy-start(bf16[4,144,256]{2,1,0:T(8,128)(2,1)} %copy.118) | copy-start | bytes 884740
  138.8 4.5 %copy-start.38 = (f32[1024]{0:T(1024)S(1)}, f32[1024]{0:T(1024)}, u32[]{:S(2)}) copy-start(f32[1024]{0:T(1024)} %param.16) | copy-start | bytes 12292
  143.3 2.8 copy-start.6
  146.0 2.5 copy-start.25
  146.0 2.5 copy-start.26
  146.0 2.5 copy-start.46
  151.7 2.6 copy-start.47
  155.3 6.1 %copy-start.48 = (f32[4,4,208]{2,1,0:T(4,128)S(1)}, f32[4,4,208]{2,1,0:T(4,128)}, u32[]{:S(2)}) copy-start(f32[4,4,208]{2,1,0:T(4,128)} %copy-done.47) | copy-start | bytes 39940
  168.3 3.0 copy-start.20
  170.8 1.2 copy-start.27
  172.0 4.1 %copy-start.8 = (bf16[1,8,128,1024]{3,2,1,0:T(8,128)(2,1)S(1)}, bf16[1,8,128,1024]{3,2,1,0:T(8,128)(2,1)}, u32[]{:S(2)}) copy-start(bf16[1,8,128,1024]{3,2,1,0:T(8,128)(2,1)} %get-tuple-element.43) | copy-start | bytes 6291460
  172.0 4.1 %copy-start.42 = (f32[4,208]{1,0:T(4,128)S(1)}, f32[4,208]{1,0:T(4,128)}, u32[]{:S(2)}) copy-start(f32[4,208]{1,0:T(4,128)} %add_rsqrt_fusion.1) | copy-start | bytes 9988
  176.1 4.8 %copy-start.21 = (bf16[4,2,1,208,1024]{4,3,2,1,0:T(8,128)(2,1)S(1)}, bf16[4,2,1,208,1024]{4,3,2,1,0:T(8,128)(2,1)}, u32[]{:S(2)}) copy-start(bf16[4,2,1,208,1024]{4,3,2,1,0:T(8,128)(2,1)} %get-tuple-element.17) | copy-start | bytes 10223620
  176.1 4.8 %copy-start.28 = (bf16[4,208,256]{2,1,0:T(8,128)(2,1)S(1)}, bf16[4,208,256]{2,1,0:T(8,128)(2,1)}, u32[]{:S(2)}) copy-start(bf16[4,208,256]{2,1,0:T(8,128)(2,1)} %copy.105) | copy-start | bytes 1277956
  176.1 4.8 %copy-start.29 = (bf16[4,208,256]{2,1,0:T(8,128)(2,1)S(1)}, bf16[4,208,256]{2,1,0:T(8,128)(2,1)}, u32[]{:S(2)}) copy-start(bf16[4,208,256]{2,1,0:T(8,128)(2,1)} %copy.103) | copy-start | bytes 1277956
  176.2 4.8 %copy-start.30 = (bf16[4,208,256]{2,1,0:T(8,128)(2,1)S(1)}, bf16[4,208,256]{2,1,0:T(8,128)(2,1)}, u32[]{:S(2)}) copy-start(bf16[4,208,256]{2,1,0:T(8,128)(2,1)} %copy.104) | copy-start | bytes 1277956
  176.2 4.8 %copy-start.36 = (f32[1024]{0:T(1024)S(1)}, f32[1024]{0:T(1024)}, u32[]{:S(2)}) copy-start(f32[1024]{0:T(1024)} %param.15) | copy-start | bytes 12292
  180.9 2.4 copy-start.45
  181.0 3.0 copy-start.13
  186.0 103.1 %copy-start.3 = (bf16[4,208,1024]{2,1,0:T(8,128)(2,1)S(1)}, bf16[4,208,1024]{2,1,0:T(8,128)(2,1)}, u32[]{:S(2)}) copy-start(bf16[4,208,1024]{2,1,0:T(8,128)(2,1)} %get-tuple-element.46) | copy-start | bytes 5111812
  186.0 103.1 %copy-start.15 = (bf16[1,8,1024]{2,1,0:T(8,128)(2,1)S(1)}, bf16[1,8,1024]{2,1,0:T(8,128)(2,1)}, u32[]{:S(2)}) copy-start(bf16[1,8,1024]{2,1,0:T(8,128)(2,1)} %param.14) | copy-start | bytes 49156
  186.0 103.1 %copy-start.40 = (f32[208]{0:T(256)S(1)}, f32[208]{0:T(256)}, u32[]{:S(2)}) copy-start(f32[208]{0:T(256)} %add_rsqrt_fusion.3) | copy-start | bytes 2500
  186.0 105.0 %copy-start.32 = (bf16[1,8,1024]{2,1,0:T(8,128)(2,1)S(1)}, bf16[1,8,1024]{2,1,0:T(8,128)(2,1)}, u32[]{:S(2)}) copy-start(bf16[1,8,1024]{2,1,0:T(8,128)(2,1)} %copy-done.31) | copy-start | bytes 49156
  287.6 3.4 %copy-start.1 = (bf16[3,1,208,1024]{3,2,1,0:T(8,128)(2,1)S(1)}, bf16[3,1,208,1024]{3,2,1,0:T(8,128)(2,1)}, u32[]{:S(2)}) copy-start(bf16[3,1,208,1024]{3,2,1,0:T(8,128)(2,1)} %get-tuple-element.21) | copy-start | bytes 3833860
  287.6 3.4 %copy-start.12 = (bf16[1,196,1024]{2,1,0:T(8,128)(2,1)S(1)}, bf16[1,196,1024]{2,1,0:T(8,128)(2,1)}, u32[]{:S(2)}) copy-start(bf16[1,196,1024]{2,1,0:T(8,128)(2,1)} %param.21) | copy-start | bytes 1204228
  289.1 2.4 copy-start.4
  289.1 2.4 copy-start.5
  289.1 2.4 copy-start.39
  289.1 2.4 copy-start.41
  291.0 1.0 copy-start.18

commit v2 on v1

--- a/solution.py
+++ b/solution.py
@@ -178,6 +178,8 @@
     G = n // R
     f, r, line, x, partner = places(n, R)
     C3 = gq.shape[3]
+    H = R // 2
+    mate = r + 1 - 2 * lax.rem(r, 2)
     greet(n, R)
     done = []
     turn = []
@@ -273,7 +275,7 @@
                 row_o.append(c)
         along_q.append(row_q)
         along_o.append(row_o)
-    spread = []
+    spread = [[], []]
     for s in range(2):
         tq = sq[s, line].astype(f32)
         to = so[s, line].astype(f32)
@@ -286,18 +288,31 @@
         fb[s, :, pl.ds(C3, oc)] = to.astype(bf16)
         fin[s, r, :, pl.ds(0, C3)] = tq.astype(bf16)
         fin[s, r, :, pl.ds(C3, oc)] = to.astype(bf16)
-        for j in range(1, R):
-            c = remote(fb.at[s], fin.at[s, r], es.at[s, j], er.at[s, j], f, lax.rem(r + j, R))
-            c.start()
-            spread.append(c)
+        for j in range(H):
+            p = lax.rem(r + 2 * j, R) if j else mate
+            c = remote(fb.at[s], fin.at[s, r], es.at[s, j], er.at[s, j], f, p)
+            c.start()
+            spread[s].append(c)
+    last = []
+    for s in range(2):
+        for j in range(1, H):
+            spread[s][j].wait_recv()
+            b = lax.rem(r - 2 * j + R, R)
+            c = remote(fin.at[s, b], fin.at[s, b], es.at[s, H - 1 + j], er.at[s, H - 1 + j], f, mate)
+            c.start()
+            last.append(c)
     for c in group_g:
         c.wait_recv()
     total = gc[0]
     for j in range(1, R):
         total = total + gc[j]
     gsum[...] = total
-    for c in back + spread:
+    for c in back + last:
         c.wait()
+    for s in range(2):
+        spread[s][0].wait_recv()
+        for c in spread[s]:
+            c.wait_send()
     for c in [cg] + line_g + group_g:
         c.wait_send()
     for s in range(2):
@@ -364,41 +379,130 @@
     return zf * inverse, inverse
 
 
-def stream(z, dyb, gain, w, wo, length):
-    clips, rows, width = z.shape
-    cols = w.shape[1] // 3
-    normed, _ = normalise(z)
-    hidden = (normed * gain).astype(bf16)
-    qkv = jnp.einsum("csd,de->cse", hidden, w, preferred_element_type=f32).astype(bf16)
+def mm(a, b, ca, cb):
+    return lax.dot_general(a, b, (((ca,), (cb,)), ((), ())), preferred_element_type=f32)
+
+
+def layer(s, length, gain, wf, wo, got, gq, go, dh, gain_out, hs, qkv_s, dqkv_s, att_s, datt_s, inv_s):
+    groups, _, per, P_, D = got.shape
+    clips = groups * per
+    rows_all = clips * P_
+    n, rows = wf.shape[1], wf.shape[2]
+    R = wo.shape[1]
+    cols = wo.shape[4]
     scale = HEAD ** (-0.5)
-    query = qkv[..., :cols].reshape(clips, rows, -1, HEAD)
-    keyed = qkv[..., cols : 2 * cols].reshape(clips, rows, -1, HEAD)
-    valued = qkv[..., 2 * cols :].reshape(clips, rows, -1, HEAD)
-    scores = jnp.einsum("cshd,cthd->chst", query, keyed, preferred_element_type=f32) * scale
-    real = lax.broadcasted_iota(jnp.int32, scores.shape, 3) < length
-    probs = jax.nn.softmax(jnp.where(real, scores, -1e30), axis=-1)
-    pb = probs.astype(bf16)
-    att = (
-        jnp.einsum("chst,cthd->cshd", pb, valued, preferred_element_type=f32)
-        .reshape(clips, rows, cols)
-        .astype(bf16)
-    )
-    out_term = jnp.einsum("csd,cse->de", att, dyb, preferred_element_type=f32).astype(bf16)
-    datt = jnp.einsum("cse,de->csd", dyb, wo, preferred_element_type=f32).astype(bf16)
-    datt = datt.reshape(clips, rows, -1, HEAD)
-    dprob = jnp.einsum("cshd,cthd->chst", datt, valued, preferred_element_type=f32)
-    dvalue = jnp.einsum("chst,cshd->cthd", pb, datt, preferred_element_type=f32)
-    dscore = probs * (dprob - jnp.sum(probs * dprob, axis=-1, keepdims=True)) * scale
-    dsb = dscore.astype(bf16)
-    dquery = jnp.einsum("chst,cthd->cshd", dsb, keyed, preferred_element_type=f32)
-    dkey = jnp.einsum("chst,cshd->cthd", dsb, query, preferred_element_type=f32)
-    dqkv = jnp.concatenate(
-        [t.astype(bf16).reshape(clips, rows, cols) for t in (dquery, dkey, dvalue)], 2
-    )
-    qkv_term = jnp.einsum("csd,cse->de", hidden, dqkv, preferred_element_type=f32).astype(bf16)
-    dhidden = jnp.einsum("cse,de->csd", dqkv, w, preferred_element_type=f32)
-    gain_term = jnp.sum(dhidden * normed, axis=(0, 1))
-    return qkv_term, out_term, dhidden.astype(bf16), gain_term
+    tile = cols
+    shards = tile // rows
+
+    def clip_step(c, _):
+        z = got[c // per, 0, lax.rem(c, per)].astype(f32)
+        inverse = lax.rsqrt(jnp.mean(z * z, axis=1, keepdims=True) + 1e-06)
+        at = pl.ds(pl.multiple_of(c * P_, 16), P_)
+        inv_s[at, :] = jnp.broadcast_to(inverse, (P_, 128))
+        hs[at, :] = (z * inverse * gain[s : s + 1, :]).astype(bf16)
+        return 0
+
+    lax.fori_loop(0, clips, clip_step, 0)
+    h = hs.at[pl.ds(0, rows_all), :]
+
+    def qkv_step(t, _):
+        at = pl.ds(pl.multiple_of(t * cols, 128), cols)
+        w = wf[s, :, :, at].reshape(n * rows, cols)
+        qkv_s[pl.ds(0, rows_all), at] = mm(h[...], w, 1, 0).astype(bf16)
+        return 0
+
+    lax.fori_loop(0, 3, qkv_step, 0)
+
+    total = jnp.zeros((rows_all, cols), f32)
+    for k in range(R):
+        dy = got[:, 1, :, :, pl.ds(k * cols, cols)].reshape(rows_all, cols)
+        total = total + mm(dy, wo[s, k].reshape(cols, cols), 1, 1)
+    datt_s[pl.ds(0, rows_all), :] = total.astype(bf16)
+
+    real = lax.broadcasted_iota(jnp.int32, (P_, P_), 1) < length
+
+    def attend(c, _):
+        at = pl.ds(pl.multiple_of(c * P_, 16), P_)
+        heads = cols // HEAD
+        qkv = qkv_s[at, :]
+        datt = datt_s[at, :]
+        att, dq, dk, dv = [], [], [], []
+        for i in range(heads):
+            q = qkv[:, i * HEAD : (i + 1) * HEAD]
+            k = qkv[:, cols + i * HEAD : cols + (i + 1) * HEAD]
+            v = qkv[:, 2 * cols + i * HEAD : 2 * cols + (i + 1) * HEAD]
+            da = datt[:, i * HEAD : (i + 1) * HEAD]
+            sc = jnp.where(real, mm(q, k, 1, 1) * scale, -1e30)
+            e = jnp.exp(sc - jnp.max(sc, axis=1, keepdims=True))
+            p = e / jnp.sum(e, axis=1, keepdims=True)
+            pb = p.astype(bf16)
+            att.append(mm(pb, v, 1, 0).astype(bf16))
+            dp = mm(da, v, 1, 1)
+            dv.append(mm(pb, da, 0, 0).astype(bf16))
+            ds = (p * (dp - jnp.sum(p * dp, axis=1, keepdims=True)) * scale).astype(bf16)
+            dq.append(mm(ds, k, 1, 0).astype(bf16))
+            dk.append(mm(ds, q, 0, 0).astype(bf16))
+        att_s[at, :] = jnp.concatenate(att, 1)
+        dqkv_s[at, :] = jnp.concatenate(dq + dk + dv, 1)
+        return 0
+
+    lax.fori_loop(0, clips, attend, 0)
+
+    def tile_step(t, _):
+        at = pl.ds(pl.multiple_of(t * tile, 128), tile)
+        dqkv = dqkv_s[pl.ds(0, rows_all), :]
+        dy = got[:, 1, :, :, at].reshape(rows_all, tile)
+        out = mm(att_s[pl.ds(0, rows_all), :], dy, 0, 0).astype(bf16)
+        go[s, :, :, at] = out.reshape(shards, rows, tile)
+        term = mm(h[:, at], dqkv, 0, 0).astype(bf16)
+        gq[s, pl.ds(t * shards, shards)] = term.reshape(shards, rows, 3 * cols)
+        w = wf[s, pl.ds(t * shards, shards), :, pl.ds(0, 3 * cols)].reshape(tile, 3 * cols)
+        d = mm(dqkv, w, 1, 1)
+        z = got[:, 0, :, :, at].reshape(rows_all, tile).astype(f32)
+        gain_out[s : s + 1, at] = jnp.sum(d * (z * inv_s[pl.ds(0, rows_all), 0:1]), axis=0, keepdims=True)
+        dh[:, :, :, at] = d.astype(bf16).reshape(groups, per, P_, tile)
+        return 0
+
+    lax.fori_loop(0, D // tile, tile_step, 0)
+
+
+def layer_scratch(rows_all, D, cols):
+    V = pltpu.VMEM
+    return [
+        V((rows_all, D), bf16),
+        V((rows_all, 3 * cols), bf16),
+        V((rows_all, 3 * cols), bf16),
+        V((rows_all, cols), bf16),
+        V((rows_all, cols), bf16),
+        V((rows_all, 128), f32),
+    ]
+
+
+def layers_kernel(lengths, wf, wo, gv, ga, gain, gq, go, dv, da, gain_out, *scratch):
+    layer(0, lengths[0], gain, wf, wo, gv, gq, go, dv, gain_out, *scratch)
+    layer(1, lengths[1], gain, wf, wo, ga, gq, go, da, gain_out, *scratch)
+
+
+def layers(lengths, wf, wo, gv, ga, gain):
+    _, n, rows, C = wf.shape
+    _, R, G, _, oc = wo.shape
+    D = gv.shape[-1]
+    vm = pl.BlockSpec(memory_space=pltpu.VMEM)
+    most = max(t.shape[0] * t.shape[2] * t.shape[3] for t in (gv, ga))
+    return pl.pallas_call(
+        functools.partial(layers_kernel, lengths),
+        out_shape=(
+            jax.ShapeDtypeStruct((2, n, rows, 3 * oc), bf16),
+            jax.ShapeDtypeStruct((2, G, rows, D), bf16),
+            jax.ShapeDtypeStruct((R,) + gv.shape[2:], bf16),
+            jax.ShapeDtypeStruct((R,) + ga.shape[2:], bf16),
+            jax.ShapeDtypeStruct((2, D), f32),
+        ),
+        in_specs=[vm] * 5,
+        out_specs=(vm,) * 5,
+        scratch_shapes=layer_scratch(most, D, oc),
+        compiler_params=pltpu.CompilerParams(vmem_limit_bytes=60 * 1024 * 1024),
+    )(wf, wo, gv, ga, gain)
 
 
 def d_rows(z, d_out, dh, gain):
@@ -447,18 +551,8 @@
 
     lengths = [t.shape[1] + bottle_in.shape[1] for t in (video_in, audio_in)]
     gains = [video_gain, audio_gain]
-    results = []
-    for s, got in enumerate((gv, ga)):
-        full = wf[s].reshape(n * rows, -1)[:, : 3 * oc]
-        rows_out = jnp.moveaxis(wo[s].reshape(R, oc, oc), 0, 1).reshape(oc, width)
-        p = got.shape[3]
-        z = got[:, 0].reshape(R * clips, p, width)
-        dy = got[:, 1].reshape(R * clips, p, width)
-        results.append(stream(z, dy, gains[s], full, rows_out, lengths[s]))
-    gq = jnp.stack([res[0].reshape(n, rows, 3 * oc) for res in results])
-    go = jnp.stack([res[1].reshape(n // R, rows, width) for res in results])
-    dhs = [res[2].reshape((R, clips) + res[2].shape[1:]) for res in results]
-    gain_terms = jnp.stack([res[3] for res in results])
+    gq, go, dv, da, gain_terms = layers(lengths, wf, wo, gv, ga, jnp.stack(gains))
+    dhs = [dv, da]
     fin, rv, ra, gsum = reduce_all(n, R, oc, gq, go, dhs[0], dhs[1], gain_terms)
     gsum = gsum / count
 

time: 307 us -> 237 us (0.77)
  matrix products: 69.9 us -> 0 us
  Pallas kernels: 175 us -> 211 us
  local copies, waits for them, and re-layouts: 38.3 us -> 12.7 us
  other arithmetic: 21.9 us -> 12.1 us
    dot_general x20 -> x0, matrix products: 62.3 us -> none  [the longest x2 11.1 us: stream(): jnp.einsum('chst,cthd->cshd', dsb, keyed, preferred_element_type=f32)]
    pallas_call x0 -> x1, Pallas kernels: none -> 39.6 us  [layers(): pl.pallas_call(functools.partial(layers_kernel, lengths), out_shape=(jax....]
    reshape x12 -> x0, local copies, waits for them, and re-layouts: 15.5 us -> none  [the longest x6 9.83 us: stream(): t.astype(bf16).reshape(clips, rows, cols)]
    sub x2 -> x0, matrix products: 7.51 us -> none  [stream(): probs = jax.nn.softmax(jnp.where(real, scores, -1e+30), axis=-1)]
    slice x7 -> x0, local copies, waits for them, and re-layouts: 7.49 us -> none  [the longest x1 4.21 us: per_device(): full = wf[s].reshape(n * rows, -1)[:, :3 * oc]]
    pallas_call x1, Pallas kernels: 102 us -> 97.9 us  [reduce_all(): pl.pallas_call(functools.partial(reduce_kernel, n, R, oc), out_shape=(jax...]
    another operation x3 -> x1, other arithmetic: 3.72 us -> 0.61 us  [per_device(): jnp.stack(gains)]
    unnamed x102 -> x44, local copies, waits for them, and re-layouts: 6.27 us -> 5.66 us
where the time goes in v2:
time: 237 us
  Pallas kernels  211 us (89%)
  local copies, waits for them, and re-layouts  12.7 us (5%)
  other arithmetic  12.1 us (5%)
    pallas_call x1, Pallas kernels, reduce_all(): pl.pallas_call(functools.partial(reduce_kernel, n, R, oc), out_shape=(jax...  97.9 us
    pallas_call x1, Pallas kernels, gather(): pl.pallas_call(functools.partial(gather_kernel, n, R, oc), out_shape=(jax...  73.6 us
    pallas_call x1, Pallas kernels, layers(): pl.pallas_call(functools.partial(layers_kernel, lengths), out_shape=(jax....  39.6 us
    unnamed x44, local copies, waits for them, and re-layouts  5.66 us

profile of v2, /device:TPU:13, one launch (start us, length us, event | category | flops | bytes accessed | tf_op | source)
XLA Modules:
  0.0 236.9 jit_solution(9223967109826221670)
XLA Ops:
  0.7 0.0 copy-start.18
  0.7 0.0 copy-start
  0.7 0.0 copy-start.6
  0.7 0.0 copy-start.8
  0.7 1.1 constant_dynamic-slice_fusion.3
  1.8 0.9 constant_dynamic-slice_fusion
  2.8 0.8 pad_maximum_fusion.2.w_ref
  3.6 0.0 copy-done.18
  3.6 0.0 copy-done
  3.6 0.0 copy-done.6
  3.6 0.0 copy-done.8
  3.6 0.0 copy-start.12
  3.7 0.0 copy-start.2
  3.7 0.0 copy-start.10
  3.7 0.1 fusion.26
  3.8 1.0 pad_maximum_fusion.tv_ref
  4.8 0.0 copy-done.12
  4.8 0.0 copy-done.2
  4.8 0.0 copy-done.10
  4.8 0.0 copy-start.14
  4.8 0.0 copy-start.16
  4.8 0.9 pad_maximum_fusion.1.ta_ref
  5.7 73.6 %shard_map.187 = (bf16[2,8,128,1024]{3,2,1,0:T(8,128)(2,1)}, bf16[2,4,2,128,256]{4,3,2,1,0:T(8,128)(2,1)}, bf16[4,2,1,208,1024]{4,3,2,1,0:T(8,128)(2,1)}, bf16[4,2,1,144,1024]{4,3,2,1,0:T(8,128)(2,1)}) custom-call(bf16[2,128,1024]{2,1,0:T(8,128)(2,1)} %pad_maximum_fusion.2.w_ref, bf16[2,1,208,1024]{3,2,1,0:T(8,128)(2,1)} %pad_maximum_fusion.tv_ref, ...), custom_call_target="tpu_custom_call" | custom-call | tf_op jit(solution)/shard_map/pallas_call | solution.py:147
  79.3 0.0 copy-done.14
  79.3 0.0 copy-done.16
  79.3 0.6 pad_maximum_fusion.3.gain
  79.9 39.6 %shard_map.188 = (bf16[2,8,128,768]{3,2,1,0:T(8,128)(2,1)}, bf16[2,2,128,1024]{3,2,1,0:T(8,128)(2,1)}, bf16[4,1,208,1024]{3,2,1,0:T(8,128)(2,1)}, bf16[4,1,144,1024]{3,2,1,0:T(8,128)(2,1)}, f32[2,1024]{1,0:T(2,128)}) custom-call(bf16[2,8,128,1024]{3,2,1,0:T(8,128)(2,1)} %get-tuple-element.22.wf, bf16[2,4,2,128,256]{4,3,2,1,0:T(8,128)(2,1)} %get-tuple-element.23.wo, ...), custom_call_target="tpu_custom_call" | custom-call | tf_op jit(solution)/shard_map/pallas_call | solution.py:492
  119.6 97.9 %shard_map.189 = (bf16[2,4,128,1024]{3,2,1,0:T(8,128)(2,1)}, bf16[3,1,208,1024]{3,2,1,0:T(8,128)(2,1)}, bf16[3,1,144,1024]{3,2,1,0:T(8,128)(2,1)}, f32[2,1024]{1,0:T(2,128)}) custom-call(bf16[2,8,128,768]{3,2,1,0:T(8,128)(2,1)} %get-tuple-element.27.gq, bf16[2,2,128,1024]{3,2,1,0:T(8,128)(2,1)} %get-tuple-element.28.go, ...), custom_call_target="tpu_custom_call" | custom-call | tf_op jit(solution)/shard_map/pallas_call | solution.py:330
  217.4 2.8 %convert_multiply_fusion = (f32[1,4,128,768]{3,2,1,0:T(8,128)}, f32[1,4,128,768]{3,2,1,0:T(8,128)S(1)}) fusion(bf16[2,4,128,1024]{3,2,1,0:T(8,128)(2,1)} %get-tuple-element.33), kind=kLoop, calls=%fused_computation | loop fusion | flops 1572864 | bytes 4718592 | tf_op jit(solution)/shard_map/div | solution.py:568
  220.2 0.5 copy.29
  220.7 0.1 copy.30
  220.8 1.6 copy.35
  222.4 1.9 copy.32
  224.3 0.1 copy.33
  224.4 0.0 copy-start.3
  224.4 0.0 copy-start.9
  224.4 0.0 copy-start.5
  224.5 0.0 copy-start.15
  224.5 1.6 copy.37
  226.1 0.0 copy-done.3
  226.1 0.0 copy-done.9
  226.1 0.1 fusion.17
  226.2 0.0 copy-done.5
  226.3 0.0 copy-done.15
  226.3 0.0 copy-start.4
  226.3 1.4 fusion.13
  227.7 0.0 copy-start.17
  227.7 0.0 copy-done.11
  227.7 0.0 copy-done.13
  227.7 1.4 fusion.16
  229.1 0.0 copy-start.7
  229.1 0.2 fusion.6
  229.3 0.4 fusion.2
  229.8 0.3 copy-done.7
  230.1 0.5 fusion.5
  230.6 0.6 fusion.28
  231.2 0.7 slice.113
  231.9 1.1 multiply_bitcast_fusion
  233.1 0.2 copy.31
  233.3 1.0 copy.36
  234.3 0.2 copy.34
  234.5 1.0 copy.38
  235.5 0.8 slice.112
  236.3 0.6 fusion.31
  (17 shorter events, 0.1 us)
Async XLA Ops:
  0.7 3.0 %copy-start.18 = (bf16[1,8,1024]{2,1,0:T(8,128)(2,1)S(1)}, bf16[1,8,1024]{2,1,0:T(8,128)(2,1)}, u32[]{:S(2)}) copy-start(bf16[1,8,1024]{2,1,0:T(8,128)(2,1)} %param.23) | copy-start | bytes 49156
  0.7 3.0 %copy-start = (bf16[1,196,1024]{2,1,0:T(8,128)(2,1)S(1)}, bf16[1,196,1024]{2,1,0:T(8,128)(2,1)}, u32[]{:S(2)}) copy-start(bf16[1,196,1024]{2,1,0:T(8,128)(2,1)} %param.12) | copy-start | bytes 1204228
  0.7 3.0 %copy-start.6 = (bf16[1,196,1024]{2,1,0:T(8,128)(2,1)S(1)}, bf16[1,196,1024]{2,1,0:T(8,128)(2,1)}, u32[]{:S(2)}) copy-start(bf16[1,196,1024]{2,1,0:T(8,128)(2,1)} %param.21) | copy-start | bytes 1204228
  0.7 3.0 %copy-start.8 = (bf16[1,8,1024]{2,1,0:T(8,128)(2,1)S(1)}, bf16[1,8,1024]{2,1,0:T(8,128)(2,1)}, u32[]{:S(2)}) copy-start(bf16[1,8,1024]{2,1,0:T(8,128)(2,1)} %param.14) | copy-start | bytes 49156
  3.6 1.1 copy-start.12
  3.7 1.1 copy-start.2
  3.7 1.1 copy-start.10
  4.8 74.5 %copy-start.14 = (f32[1024]{0:T(1024)S(1)}, f32[1024]{0:T(1024)}, u32[]{:S(2)}) copy-start(f32[1024]{0:T(1024)} %param.16) | copy-start | bytes 12292
  4.8 74.5 %copy-start.16 = (f32[1024]{0:T(1024)S(1)}, f32[1024]{0:T(1024)}, u32[]{:S(2)}) copy-start(f32[1024]{0:T(1024)} %param.15) | copy-start | bytes 12292
  224.4 1.7 copy-start.3
  224.4 1.7 copy-start.9
  224.4 1.8 copy-start.5
  224.5 1.8 copy-start.15
  226.1 1.6 copy-start.11
  226.1 1.6 copy-start.13
  226.3 3.0 %copy-start.4 = (bf16[4,1,208,1024]{3,2,1,0:T(8,128)(2,1)S(1)}, bf16[4,1,208,1024]{3,2,1,0:T(8,128)(2,1)}, u32[]{:S(2)}) copy-start(bf16[4,1,208,1024]{3,2,1,0:T(8,128)(2,1)} %get-tuple-element.26.dv) | copy-start | bytes 5111812
  227.7 1.6 copy-start.1
  227.7 1.6 copy-start.17
  229.1 1.0 copy-start.7
  234.3 2.0 copy-start.19

commit v3 on v0

v3 whole, which is shorter than its diff:
```python
import functools

import jax
import jax.numpy as jnp
from jax import lax
from jax.experimental import pallas as pl
from jax.experimental.pallas import tpu as pltpu
from jax.sharding import PartitionSpec as P

HEAD = 64
f32 = jnp.float32
bf16 = jnp.bfloat16


def remote(src, dst, send, recv, f, r):
    return pltpu.make_async_remote_copy(
        src_ref=src,
        dst_ref=dst,
        send_sem=send,
        recv_sem=recv,
        device_id={"fsdp": f, "rep": r},
        device_id_type=pl.DeviceIdType.MESH,
    )


def places(n, R):
    f = lax.axis_index("fsdp")
    r = lax.axis_index("rep")
    line = f // 2
    x = lax.rem(f, 2)
    return f, r, line, x, f + 1 - 2 * x


def greet(n, R):
    f, r, line, x, partner = places(n, R)
    barrier = pltpu.get_barrier_semaphore()

    def signal(ff, rr):
        pl.semaphore_signal(
            barrier,
            inc=1,
            device_id={"fsdp": ff, "rep": rr},
            device_id_type=pl.DeviceIdType.MESH,
        )

    signal(partner, r)
    for j in range(1, n // 2):
        signal(lax.rem(line + j, n // 2) * 2 + x, r)
    for j in range(1, R):
        signal(f, lax.rem(r + j, R))
    pl.semaphore_wait(barrier, n // 2 + R - 1)


def mm(a, b, ca, cb):
    return lax.dot_general(a, b, (((ca,), (cb,)), ((), ())), preferred_element_type=f32)


def layer(s, length, gain, wf, wo, got, gq, go, dh, gain_out, hs, qkv_s, dqkv_s, att_s, datt_s, inv_s, early, late):
    groups, _, per, P_, D = got.shape
    clips = groups * per
    rows_all = clips * P_
    n, rows = wf.shape[1], wf.shape[2]
    R = wo.shape[1]
    cols = wo.shape[4]
    scale = HEAD ** (-0.5)
    tile = cols
    shards = tile // rows

    def clip_step(c, _):
        z = got[c // per, 0, lax.rem(c, per)].astype(f32)
        inverse = lax.rsqrt(jnp.mean(z * z, axis=1, keepdims=True) + 1e-06)
        at = pl.ds(pl.multiple_of(c * P_, 16), P_)
        inv_s[at, :] = jnp.broadcast_to(inverse, (P_, 128))
        hs[at, :] = (z * inverse * gain[s : s + 1, :]).astype(bf16)
        return 0

    lax.fori_loop(0, clips, clip_step, 0)
    h = hs.at[pl.ds(0, rows_all), :]

    def qkv_step(t, _):
        at = pl.ds(pl.multiple_of(t * cols, 128), cols)
        w = wf[s, :, :, at].reshape(n * rows, cols)
        qkv_s[pl.ds(0, rows_all), at] = mm(h[...], w, 1, 0).astype(bf16)
        return 0

    lax.fori_loop(0, 3, qkv_step, 0)
    early()

    total = jnp.zeros((rows_all, cols), f32)
    for k in range(R):
        dy = got[:, 1, :, :, pl.ds(k * cols, cols)].reshape(rows_all, cols)
        total = total + mm(dy, wo[s, k].reshape(cols, cols), 1, 1)
    datt_s[pl.ds(0, rows_all), :] = total.astype(bf16)

    real = lax.broadcasted_iota(jnp.int32, (P_, P_), 1) < length

    def attend(c, _):
        at = pl.ds(pl.multiple_of(c * P_, 16), P_)
        heads = cols // HEAD
        qkv = qkv_s[at, :]
        datt = datt_s[at, :]
        att, dq, dk, dv = [], [], [], []
        for i in range(heads):
            q = qkv[:, i * HEAD : (i + 1) * HEAD]
            k = qkv[:, cols + i * HEAD : cols + (i + 1) * HEAD]
            v = qkv[:, 2 * cols + i * HEAD : 2 * cols + (i + 1) * HEAD]
            da = datt[:, i * HEAD : (i + 1) * HEAD]
            sc = jnp.where(real, mm(q, k, 1, 1) * scale, -1e30)
            e = jnp.exp(sc - jnp.max(sc, axis=1, keepdims=True))
            p = e / jnp.sum(e, axis=1, keepdims=True)
            pb = p.astype(bf16)
            att.append(mm(pb, v, 1, 0).astype(bf16))
            dp = mm(da, v, 1, 1)
            dv.append(mm(pb, da, 0, 0).astype(bf16))
            ds = (p * (dp - jnp.sum(p * dp, axis=1, keepdims=True)) * scale).astype(bf16)
            dq.append(mm(ds, k, 1, 0).astype(bf16))
            dk.append(mm(ds, q, 0, 0).astype(bf16))
        att_s[at, :] = jnp.concatenate(att, 1)
        dqkv_s[at, :] = jnp.concatenate(dq + dk + dv, 1)
        return 0

    lax.fori_loop(0, clips, attend, 0)
    late()

    def tile_step(t, _):
        at = pl.ds(pl.multiple_of(t * tile, 128), tile)
        dqkv = dqkv_s[pl.ds(0, rows_all), :]
        dy = got[:, 1, :, :, at].reshape(rows_all, tile)
        out = mm(att_s[pl.ds(0, rows_all), :], dy, 0, 0).astype(bf16)
        go[s, :, :, at] = out.reshape(shards, rows, tile)
        term = mm(h[:, at], dqkv, 0, 0).astype(bf16)
        gq[s, pl.ds(t * shards, shards)] = term.reshape(shards, rows, 3 * cols)
        w = wf[s, pl.ds(t * shards, shards), :, pl.ds(0, 3 * cols)].reshape(tile, 3 * cols)
        d = mm(dqkv, w, 1, 1)
        z = got[:, 0, :, :, at].reshape(rows_all, tile).astype(f32)
        gain_out[s : s + 1, at] = jnp.sum(d * (z * inv_s[pl.ds(0, rows_all), 0:1]), axis=0, keepdims=True)
        dh[:, :, :, at] = d.astype(bf16).reshape(groups, per, P_, tile)
        return 0

    lax.fori_loop(0, D // tile, tile_step, 0)


def layer_scratch(rows_all, D, cols):
    V = pltpu.VMEM
    return [
        V((rows_all, D), bf16),
        V((rows_all, 3 * cols), bf16),
        V((rows_all, 3 * cols), bf16),
        V((rows_all, cols), bf16),
        V((rows_all, cols), bf16),
        V((rows_all, 128), f32),
    ]


def kernel(n, R, oc, lengths, count, w_ref, tv_ref, ta_ref, gain_ref,
           dzv, dza, qv, ov, qa, oa, gsum,
           wf, wo, gv, ga, gq, go, dv, da, hs, qkv_s, dqkv_s, att_s, datt_s, inv_s,
           fin, rv, ra, ob, xq, xo, sq, so, zq, zo, fb, gain, gx, gb, gc,
           zs, zr, xs, xr, ts, tr, os, orr,
           as_, ar, qs, qr, ps, pr, us, ur, vs, vr, es, er, ds_, dr, ks, kr, loc):
    L = n // 2
    G = n // R
    H = R // 2
    f, r, line, x, partner = places(n, R)
    mate = r + 1 - 2 * lax.rem(r, 2)
    C = w_ref.shape[2]
    C3 = C - oc
    greet(n, R)
    pending = []

    def go_(c):
        c.start()
        pending.append(c)
        return c

    srcs, gots, dhs, backs = (tv_ref, ta_ref), (gv, ga), (dv, da), (rv, ra)
    own = [pltpu.make_async_copy(w_ref.at[s], wf.at[s, f], loc.at[s]) for s in range(2)]
    own_t = [pltpu.make_async_copy(srcs[s], gots[s].at[r], loc.at[2 + s]) for s in range(2)]
    along, across, tokens, relay = [[], []], [[], []], [[], []], [[], []]
    for s in range(2):
        for j in range(1, L):
            p = lax.rem(line + j, L) * 2 + x
            along[s].append(go_(remote(w_ref.at[s], wf.at[s, f], zs.at[s, j], zr.at[s, j], p, r)))
        across[s].append(go_(remote(w_ref.at[s], wf.at[s, f], xs.at[s, 0], xr.at[s, 0], partner, r)))
        for j in range(1, H):
            p = lax.rem(r + 2 * j, R)
            tokens[s].append(go_(remote(srcs[s], gots[s].at[r], ts.at[s, j], tr.at[s, j], f, p)))
        relay[s].append(go_(remote(srcs[s], gots[s].at[r], ts.at[s, 0], tr.at[s, 0], f, mate)))
    for c in own + own_t:
        c.start()

    def forward(s):
        got = gots[s]
        for j in range(1, L):
            along[s][j - 1].wait_recv()
            b = lax.rem(line - j + L, L) * 2 + x
            across[s].append(go_(remote(wf.at[s, b], wf.at[s, b], xs.at[s, j], xr.at[s, j], partner, r)))
        for j in range(1, H):
            tokens[s][j - 1].wait_recv()
            b = lax.rem(r - 2 * j + R, R)
            k = H - 1 + j
            relay[s].append(go_(remote(got.at[b], got.at[b], ts.at[s, k], tr.at[s, k], f, mate)))

    def exchange_out(s):
        own[s].wait()
        for c in across[s]:
            c.wait_recv()
        swap = []
        for j in range(1, R):
            p = lax.rem(r + j, R)
            src = wf.at[s, pl.ds(p * G, G), :, pl.ds(C3, oc)]
            swap.append(go_(remote(src, wo.at[s, r], os.at[s, j], orr.at[s, j], f, p)))
        c = pltpu.make_async_copy(wf.at[s, pl.ds(r * G, G), :, pl.ds(C3, oc)], wo.at[s, r], loc.at[4 + s])
        c.start()
        own_t[s].wait()
        for k in relay[s]:
            k.wait_recv()
        return swap, c

    def arrived(swap, c):
        c.wait()
        for k in swap:
            k.wait_recv()

    turn, cross_q, cross_o, back = [[], []], [[], []], [[], []], [[], []]
    along_q, along_o, spread, last = [[], []], [[], []], [[], []], [[], []]
    own_o = [
        pltpu.make_async_copy(
            go.at[s, :, :, pl.ds(pl.multiple_of(r * oc, oc), oc)], ob.at[s, pl.ds(r * G, G)], loc.at[6 + s]
        )
        for s in range(2)
    ]

    def reduce_1(s):
        for j in range(1, R):
            p = lax.rem(r + j, R)
            src = go.at[s, :, :, pl.ds(pl.multiple_of(p * oc, oc), oc)]
            turn[s].append(go_(remote(src, ob.at[s, pl.ds(r * G, G)], as_.at[s, j], ar.at[s, j], f, p)))
        own_o[s].start()
        for k in list(range(1, L)) + [0]:
            j = lax.rem(line + k, L)
            c = remote(gq.at[s, 2 * j + 1 - x], xq.at[s, j], qs.at[s, k], qr.at[s, k], partner, r)
            cross_q[s].append(go_(c))
        for j in range(1, R):
            p = lax.rem(r + j, R)
            back[s].append(go_(remote(dhs[s].at[p], backs[s].at[j - 1], ds_.at[s, j], dr.at[s, j], f, p)))

    def reduce_2(s):
        own_o[s].wait()
        for c in turn[s]:
            c.wait_recv()
        for k in list(range(1, L)) + [0]:
            j = lax.rem(line + k, L)
            c = remote(ob.at[s, 2 * j + 1 - x], xo.at[s, j], ps.at[s, k], pr.at[s, k], partner, r)
            cross_o[s].append(go_(c))

    def reduce_3(s):
        for i, k in enumerate(list(range(1, L)) + [0]):
            j = lax.rem(line + k, L)
            cross_q[s][i].wait_recv()
            sq[s, j] = (gq[s, 2 * j + x].astype(f32) + xq[s, j].astype(f32)).astype(bf16)
            if k:
                c = remote(sq.at[s, j], zq.at[s, k - 1], us.at[s, k], ur.at[s, k], 2 * j + x, r)
                along_q[s].append(go_(c))
        for i, k in enumerate(list(range(1, L)) + [0]):
            j = lax.rem(line + k, L)
            cross_o[s][i].wait_recv()
            so[s, j] = (ob[s, 2 * j + x].astype(f32) + xo[s, j].astype(f32)).astype(bf16)
            if k:
                c = remote(so.at[s, j], zo.at[s, k - 1], vs.at[s, k], vr.at[s, k], 2 * j + x, r)
                along_o[s].append(go_(c))

    def reduce_4(s):
        tq = sq[s, line].astype(f32)
        for k in range(1, L):
            along_q[s][k - 1].wait_recv()
            tq = tq + zq[s, k - 1].astype(f32)
        fb[s, :, pl.ds(0, C3)] = tq.astype(bf16)
        to = so[s, line].astype(f32)
        for k in range(1, L):
            along_o[s][k - 1].wait_recv()
            to = to + zo[s, k - 1].astype(f32)
        fb[s, :, pl.ds(C3, oc)] = to.astype(bf16)
        fin[s, r] = fb[s]
        for j in range(H):
            p = lax.rem(r + 2 * j, R) if j else mate
            spread[s].append(go_(remote(fb.at[s], fin.at[s, r], es.at[s, j], er.at[s, j], f, p)))

    def reduce_5(s):
        for j in range(1, H):
            spread[s][j].wait_recv()
            b = lax.rem(r - 2 * j + R, R)
            k = H - 1 + j
            last[s].append(go_(remote(fin.at[s, b], fin.at[s, b], es.at[s, k], er.at[s, k], f, mate)))

    def rows_back(s, dz):
        for c in back[s]:
            c.wait_recv()
        for i in range(dz.shape[0]):
            dh = dhs[s][r, i].astype(f32)
            for j in range(R - 1):
                dh = dh + backs[s][j, i].astype(f32)
            z = srcs[s][0, i].astype(f32)
            inverse = lax.rsqrt(jnp.mean(z * z, axis=1, keepdims=True) + 1e-06)
            normed = z * inverse
            dnorm = dh * gain_ref[s : s + 1, :]
            mean = jnp.mean(dnorm * normed, axis=1, keepdims=True)
            dz[i] = srcs[s][1, i].astype(f32) + inverse * (dnorm - normed * mean)

    def finish(s, q_out, o_out):
        spread[s][0].wait_recv()
        for c in last[s]:
            c.wait_recv()
        width = R * oc
        for g in range(R):
            for k in range(3):
                part = fin[s, g, :, pl.ds(k * oc, oc)].astype(f32) / count
                q_out[:, pl.ds(k * width + g * oc, oc)] = part
            o_out[:, pl.ds(g * oc, oc)] = fin[s, g, :, pl.ds(C3, oc)].astype(f32) / count

    def nothing():
        pass

    work = (hs, qkv_s, dqkv_s, att_s, datt_s, inv_s)
    forward(0)
    arrived(*exchange_out(0))
    layer(0, lengths[0], gain_ref, wf, wo, gv, gq, go, dv, gain, *work, nothing, functools.partial(forward, 1))
    reduce_1(0)
    arrived(*exchange_out(1))
    layer(1, lengths[1], gain_ref, wf, wo, ga, gq, go, da, gain, *work,
          functools.partial(reduce_2, 0), functools.partial(reduce_3, 0))
    reduce_1(1)
    cg = go_(remote(gain, gx, ks.at[0], kr.at[0], partner, r))
    reduce_4(0)
    cg.wait_recv()
    gb[line] = gain[...] + gx[...]
    line_g = []
    for j in range(1, L):
        p = lax.rem(line + j, L) * 2 + x
        line_g.append(go_(remote(gb.at[line], gb.at[line], ks.at[j], kr.at[j], p, r)))
    reduce_2(1)
    rows_back(0, dzv)
    for c in line_g:
        c.wait_recv()
    total = gb[0]
    for j in range(1, L):
        total = total + gb[j]
    gc[r] = total
    group_g = []
    for j in range(1, R):
        p = lax.rem(r + j, R)
        group_g.append(go_(remote(gc.at[r], gc.at[r], ks.at[L + j], kr.at[L + j], f, p)))
    reduce_3(1)
    reduce_5(0)
    rows_back(1, dza)
    for c in group_g:
        c.wait_recv()
    total = gc[0]
    for j in range(1, R):
        total = total + gc[j]
    gsum[...] = total / count
    reduce_4(1)
    finish(0, qv, ov)
    reduce_5(1)
    finish(1, qa, oa)
    for c in pending:
        c.wait_send()


def run(n, R, oc, lengths, count, w, tv, ta, gain):
    _, rows, C = w.shape
    C3 = C - oc
    D = tv.shape[-1]
    L, G, H = n // 2, n // R, R // 2
    dma = pltpu.SemaphoreType.DMA
    V = pltpu.VMEM
    vm = pl.BlockSpec(memory_space=pltpu.VMEM)
    S = jax.ShapeDtypeStruct
    most = max(R * t.shape[1] * t.shape[2] for t in (tv, ta))
    buffers = [
        V((2, n, rows, C), bf16),
        V((2, R, G, rows, oc), bf16),
        V((R,) + tv.shape, bf16),
        V((R,) + ta.shape, bf16),
        V((2, n, rows, C3), bf16),
        V((2, G, rows, D), bf16),
        V((R,) + tv.shape[1:], bf16),
        V((R,) + ta.shape[1:], bf16),
        *layer_scratch(most, D, oc),
        V((2, R, rows, C), bf16),
        V((R - 1,) + tv.shape[1:], bf16),
        V((R - 1,) + ta.shape[1:], bf16),
        V((2, n, rows, oc), bf16),
        V((2, L, rows, C3), bf16),
        V((2, L, rows, oc), bf16),
        V((2, L, rows, C3), bf16),
        V((2, L, rows, oc), bf16),
        V((2, L - 1, rows, C3), bf16),
        V((2, L - 1, rows, oc), bf16),
        V((2, rows, C), bf16),
        V((2, D), f32),
        V((2, D), f32),
        V((L, 2, D), f32),
        V((R, 2, D), f32),
    ]
    sizes = [L, L, 2 * H, R, R, L, L, L, L, R, R]
    sems = []
    for k in sizes:
        sems += [dma((2, k)), dma((2, k))]
    sems += [dma((L + R,)), dma((L + R,)), dma((8,))]
    return pl.pallas_call(
        functools.partial(kernel, n, R, oc, lengths, count),
        out_shape=(
            S(tv.shape[1:], f32),
            S(ta.shape[1:], f32),
            S((rows, 3 * D), f32),
            S((rows, D), f32),
            S((rows, 3 * D), f32),
            S((rows, D), f32),
            S((2, D), f32),
        ),
        in_specs=[vm] * 4,
        out_specs=(vm,) * 7,
        scratch_shapes=buffers + sems,
        compiler_params=pltpu.CompilerParams(
            collective_id=0, has_side_effects=True, vmem_limit_bytes=62 * 1024 * 1024
        ),
    )(w, tv, ta, gain)


def padded(tokens, bottle):
    rows = tokens.shape[1] + bottle.shape[1]
    return jnp.pad(jnp.concatenate([tokens, bottle], 1), ((0, 0), (0, -rows % 16), (0, 0)))


def per_device(
    n,
    R,
    video_in,
    audio_in,
    bottle_in,
    video_gain,
    audio_gain,
    video_qkv,
    video_out,
    audio_qkv,
    audio_out,
    grad_video,
    grad_audio,
    grad_bottle,
):
    r = lax.axis_index("rep")
    clips = video_in.shape[0]
    count = float(clips * n * R)
    rows, width = video_out.shape
    oc = width // R

    def quarter(qkv, out):
        parts = [lax.dynamic_slice_in_dim(qkv, k * width + r * oc, oc, 1) for k in range(3)]
        return jnp.concatenate(parts + [lax.dynamic_slice_in_dim(out, r * oc, oc, 1)], 1)

    w = jnp.stack([quarter(video_qkv, video_out), quarter(audio_qkv, audio_out)])
    half = (grad_bottle.astype(f32) * 0.5).astype(bf16)
    zs = [padded(video_in, bottle_in), padded(audio_in, bottle_in)]
    dys = [padded(grad_video, half), padded(grad_audio, half)]
    tv, ta = [jnp.stack([z, dy]) for z, dy in zip(zs, dys)]
    lengths = [t.shape[1] + bottle_in.shape[1] for t in (video_in, audio_in)]
    gains = jnp.stack([video_gain, audio_gain])
    dzv, dza, qv, ov, qa, oa, gsum = run(n, R, oc, lengths, count, w, tv, ta, gains)
    tv_len, ta_len = video_in.shape[1], audio_in.shape[1]
    dbottle = dzv[:, tv_len : lengths[0]] + dza[:, ta_len : lengths[1]]
    return (
        dzv[:, :tv_len].astype(bf16),
        dza[:, :ta_len].astype(bf16),
        dbottle.astype(bf16),
        qv,
        ov,
        qa,
        oa,
        gsum[0],
        gsum[1],
    )


def solution(mesh):
    n = mesh.shape["fsdp"]
    R = mesh.shape["rep"]
    clip = P(("fsdp", "rep"), None, None)
    shard = P("fsdp", None)
    in_specs = (clip, clip, clip, P(), P(), shard, shard, shard, shard, clip, clip, clip)
    out_specs = (clip, clip, clip, shard, shard, shard, shard, P(), P())
    return jax.shard_map(
        functools.partial(per_device, n, R),
        mesh=mesh,
        in_specs=in_specs,
        out_specs=out_specs,
        check_vma=False,
    )
```

time: 718 us -> 196 us (0.27)
  waiting for transfers between devices: 467 us -> 0 us
  Pallas kernels: 0 us -> 174 us
  blocking collectives: 131 us -> 0 us
  matrix products: 84.5 us -> 0 us
  between operations: 14.3 us -> 0.73 us
    reduce_scatter x8 -> x0, waiting for transfers between devices: 340 us -> none  [the longest x2 114 us: reduce_grads(): lax.psum_scatter(qkv_term.astype(jnp.bfloat16), 'rep', scatter_dimension=...]
    pallas_call x0 -> x1, Pallas kernels: none -> 174 us  [run(): pl.pallas_call(functools.partial(kernel, n, R, oc, lengths, count), out_s...]
    all_gather x6 -> x0, waiting for transfers between devices: 127 us -> none  [the longest x2 89.3 us: fetch(): lax.all_gather(qkv_part, 'fsdp', axis=0, tiled=True)]
    all_gather x6 -> x0, blocking collectives: 90.2 us -> none  [the longest x2 52.1 us: fetch(): lax.all_gather(out_part, 'fsdp', axis=0, tiled=True)]
    dot_general x20 -> x0, matrix products: 78 us -> none  [the longest x2 13.6 us: stream(): dkey = jnp.einsum('hst,shd->thd', dsb, query, preferred_element_type=f32)]
    psum x1 -> x0, blocking collectives: 40.4 us -> none  [per_device(): lax.psum((video_sums[2], audio_sums[2]), ('fsdp', 'rep'))]
  transfers between devices with their start and end apart: 14 -> 0, of which waited for: 12 -> 0; matrix products, arithmetic and copies ran while one was open for 14% -> 0% of each run, Pallas kernels for 0% -> 0%
where the time goes in v3:
time: 196 us; the launch traced here: 194 us
  Pallas kernels  174 us (89%)
  local copies, waits for them, and re-layouts  13 us (7%)
  other arithmetic  6.36 us (3%)
    pallas_call x1, Pallas kernels, run(): pl.pallas_call(functools.partial(kernel, n, R, oc, lengths, count), out_s...  174 us
    unnamed x20, local copies, waits for them, and re-layouts  5.87 us

profile of v3, /device:TPU:13, one launch (start us, length us, event | category | flops | bytes accessed | tf_op | source)
XLA Modules:
  0.0 194.0 jit_solution(7582287939270370842)
XLA Ops:
  0.6 1.3 pad_maximum_fusion.3.gain_ref
  2.0 0.7 multiply_convert_fusion
  2.7 0.0 copy-start.5
  2.7 0.0 copy-start.6
  2.7 0.0 copy-start.7
  2.7 0.9 constant_dynamic-slice_fusion
  3.6 1.0 constant_dynamic-slice_fusion.3
  4.8 0.0 copy-start.3
  4.8 0.0 copy-start.4
  4.8 0.8 pad_maximum_fusion.2.w_ref
  5.6 0.0 copy-done.5
  5.6 0.0 copy-done.6
  5.6 0.0 copy-done.7
  5.7 0.9 pad_maximum_fusion.1.ta_ref
  6.5 0.0 copy-done.3
  6.5 0.0 copy-done.4
  6.5 0.1 fusion.9
  6.6 1.0 pad_maximum_fusion.tv_ref
  7.6 174.0 %shard_map.187 = (f32[1,208,1024]{2,1,0:T(8,128)}, f32[1,144,1024]{2,1,0:T(8,128)}, f32[128,3072]{1,0:T(8,128)}, f32[128,1024]{1,0:T(8,128)}, f32[128,3072]{1,0:...) custom-call(bf16[2,128,1024]{2,1,0:T(8,128)(2,1)} %pad_maximum_fusion.2.w_ref, ...), custom_call_target="tpu_custom_call" | custom-call | tf_op jit(solution)/shard_map/pallas_call | solution.py:411
  181.6 1.4 fusion.16
  183.0 1.5 add_convert_fusion
  184.4 2.0 %slice.32 = bf16[1,196,1024]{2,1,0:T(8,128)(2,1)} slice(f32[1,208,1024]{2,1,0:T(8,128)} %get-tuple-element.16), slice={[0:1], [0:196], [0:1024]} | slice | bytes 802816 | tf_op jit(solution)/shard_map/slice | solution.py:473
  186.4 1.8 slice.33
  188.2 0.0 copy-start.2
  188.2 0.0 copy-start
  188.2 2.8 %copy.25 = f32[128,3072]{1,0:T(8,128)} copy(f32[128,3072]{1,0:T(8,128)} %get-tuple-element.52) | data formatting | bytes 3145728
  191.0 0.0 copy-done.2
  191.0 0.8 copy.26
  191.8 0.0 copy-done
  191.8 0.0 copy-start.1
  191.8 1.1 copy.27
  193.0 0.3 copy-done.1
  193.2 0.8 copy.28
  (3 shorter events, 0.1 us)
Async XLA Ops:
  2.7 2.9 %copy-start.5 = (bf16[1,128,1024]{2,1,0:T(8,128)(2,1)S(1)}, bf16[1,128,1024]{2,1,0:T(8,128)(2,1)}, u32[]{:S(2)}) copy-start(bf16[1,128,1024]{2,1,0:T(8,128)(2,1)} %param.13) | copy-start | bytes 786436
  2.7 2.9 %copy-start.6 = (bf16[1,128,1024]{2,1,0:T(8,128)(2,1)S(1)}, bf16[1,128,1024]{2,1,0:T(8,128)(2,1)}, u32[]{:S(2)}) copy-start(bf16[1,128,1024]{2,1,0:T(8,128)(2,1)} %param.22) | copy-start | bytes 786436
  2.7 2.9 %copy-start.7 = (bf16[1,8,1024]{2,1,0:T(8,128)(2,1)S(1)}, bf16[1,8,1024]{2,1,0:T(8,128)(2,1)}, u32[]{:S(2)}) copy-start(bf16[1,8,1024]{2,1,0:T(8,128)(2,1)} %param.14) | copy-start | bytes 49156
  4.8 1.8 copy-start.3
  4.8 1.8 copy-start.4
  188.2 2.9 %copy-start.2 = (f32[128,1024]{1,0:T(8,128)S(1)}, f32[128,1024]{1,0:T(8,128)}, u32[]{:S(2)}) copy-start(f32[128,1024]{1,0:T(8,128)} %get-tuple-element.53) | copy-start | bytes 1572868
  188.2 3.7 %copy-start = (f32[128,3072]{1,0:T(8,128)S(1)}, f32[128,3072]{1,0:T(8,128)}, u32[]{:S(2)}) copy-start(f32[128,3072]{1,0:T(8,128)} %get-tuple-element.54) | copy-start | bytes 4718596
  191.8 1.4 copy-start.1

commit v4 on v3

--- a/solution.py
+++ b/solution.py
@@ -153,7 +153,7 @@
 
 
 def kernel(n, R, oc, lengths, count, w_ref, tv_ref, ta_ref, gain_ref,
-           dzv, dza, qv, ov, qa, oa, gsum,
+           dzv, dza, dzb, qv, ov, qa, oa, gsum,
            wf, wo, gv, ga, gq, go, dv, da, hs, qkv_s, dqkv_s, att_s, datt_s, inv_s,
            fin, rv, ra, ob, xq, xo, sq, so, zq, zo, fb, gain, gx, gb, gc,
            zs, zr, xs, xr, ts, tr, os, orr,
@@ -177,11 +177,17 @@
     own = [pltpu.make_async_copy(w_ref.at[s], wf.at[s, f], loc.at[s]) for s in range(2)]
     own_t = [pltpu.make_async_copy(srcs[s], gots[s].at[r], loc.at[2 + s]) for s in range(2)]
     along, across, tokens, relay = [[], []], [[], []], [[], []], [[], []]
+
+    def own_across(s):
+        c = remote(w_ref.at[s], wf.at[s, f], xs.at[s, 0], xr.at[s, 0], partner, r)
+        across[s].append(go_(c))
+
     for s in range(2):
         for j in range(1, L):
             p = lax.rem(line + j, L) * 2 + x
             along[s].append(go_(remote(w_ref.at[s], wf.at[s, f], zs.at[s, j], zr.at[s, j], p, r)))
-        across[s].append(go_(remote(w_ref.at[s], wf.at[s, f], xs.at[s, 0], xr.at[s, 0], partner, r)))
+        if s == 0:
+            own_across(s)
         for j in range(1, H):
             p = lax.rem(r + 2 * j, R)
             tokens[s].append(go_(remote(srcs[s], gots[s].at[r], ts.at[s, j], tr.at[s, j], f, p)))
@@ -293,10 +299,12 @@
             k = H - 1 + j
             last[s].append(go_(remote(fin.at[s, b], fin.at[s, b], es.at[s, k], er.at[s, k], f, mate)))
 
-    def rows_back(s, dz):
+    def rows_back(s, out):
+        own_rows = out.shape[1]
+        nb = lengths[s] - own_rows
         for c in back[s]:
             c.wait_recv()
-        for i in range(dz.shape[0]):
+        for i in range(out.shape[0]):
             dh = dhs[s][r, i].astype(f32)
             for j in range(R - 1):
                 dh = dh + backs[s][j, i].astype(f32)
@@ -305,7 +313,9 @@
             normed = z * inverse
             dnorm = dh * gain_ref[s : s + 1, :]
             mean = jnp.mean(dnorm * normed, axis=1, keepdims=True)
-            dz[i] = srcs[s][1, i].astype(f32) + inverse * (dnorm - normed * mean)
+            dz = srcs[s][1, i].astype(f32) + inverse * (dnorm - normed * mean)
+            out[i] = dz[:own_rows].astype(bf16)
+            dzb[s, i] = dz[own_rows : own_rows + nb]
 
     def finish(s, q_out, o_out):
         spread[s][0].wait_recv()
@@ -323,12 +333,23 @@
 
     work = (hs, qkv_s, dqkv_s, att_s, datt_s, inv_s)
     forward(0)
-    arrived(*exchange_out(0))
-    layer(0, lengths[0], gain_ref, wf, wo, gv, gq, go, dv, gain, *work, nothing, functools.partial(forward, 1))
+    own_across(1)
+    swap_0 = exchange_out(0)
+
+    def early_0():
+        arrived(*swap_0)
+        forward(1)
+
+    layer(0, lengths[0], gain_ref, wf, wo, gv, gq, go, dv, gain, *work, early_0, nothing)
     reduce_1(0)
-    arrived(*exchange_out(1))
+    swap_1 = exchange_out(1)
+
+    def early_1():
+        arrived(*swap_1)
+        reduce_2(0)
+
     layer(1, lengths[1], gain_ref, wf, wo, ga, gq, go, da, gain, *work,
-          functools.partial(reduce_2, 0), functools.partial(reduce_3, 0))
+          early_1, functools.partial(reduce_3, 0))
     reduce_1(1)
     cg = go_(remote(gain, gx, ks.at[0], kr.at[0], partner, r))
     reduce_4(0)
@@ -367,7 +388,7 @@
         c.wait_send()
 
 
-def run(n, R, oc, lengths, count, w, tv, ta, gain):
+def run(n, R, oc, lengths, own_rows, count, w, tv, ta, gain):
     _, rows, C = w.shape
     C3 = C - oc
     D = tv.shape[-1]
@@ -376,6 +397,7 @@
     V = pltpu.VMEM
     vm = pl.BlockSpec(memory_space=pltpu.VMEM)
     S = jax.ShapeDtypeStruct
+    clips = tv.shape[1]
     most = max(R * t.shape[1] * t.shape[2] for t in (tv, ta))
     buffers = [
         V((2, n, rows, C), bf16),
@@ -411,8 +433,8 @@
     return pl.pallas_call(
         functools.partial(kernel, n, R, oc, lengths, count),
         out_shape=(
-            S(tv.shape[1:], f32),
-            S(ta.shape[1:], f32),
+            *(S((clips, t, D), bf16) for t in own_rows),
+            S((2, clips, lengths[0] - own_rows[0], D), f32),
             S((rows, 3 * D), f32),
             S((rows, D), f32),
             S((rows, 3 * D), f32),
@@ -420,7 +442,7 @@
             S((2, D), f32),
         ),
         in_specs=[vm] * 4,
-        out_specs=(vm,) * 7,
+        out_specs=(vm,) * 8,
         scratch_shapes=buffers + sems,
         compiler_params=pltpu.CompilerParams(
             collective_id=0, has_side_effects=True, vmem_limit_bytes=62 * 1024 * 1024
@@ -466,13 +488,12 @@
     tv, ta = [jnp.stack([z, dy]) for z, dy in zip(zs, dys)]
     lengths = [t.shape[1] + bottle_in.shape[1] for t in (video_in, audio_in)]
     gains = jnp.stack([video_gain, audio_gain])
-    dzv, dza, qv, ov, qa, oa, gsum = run(n, R, oc, lengths, count, w, tv, ta, gains)
-    tv_len, ta_len = video_in.shape[1], audio_in.shape[1]
-    dbottle = dzv[:, tv_len : lengths[0]] + dza[:, ta_len : lengths[1]]
+    own_rows = (video_in.shape[1], audio_in.shape[1])
+    dzv, dza, dzb, qv, ov, qa, oa, gsum = run(n, R, oc, lengths, own_rows, count, w, tv, ta, gains)
     return (
-        dzv[:, :tv_len].astype(bf16),
-        dza[:, :ta_len].astype(bf16),
-        dbottle.astype(bf16),
+        dzv,
+        dza,
+        (dzb[0] + dzb[1]).astype(bf16),
         qv,
         ov,
         qa,

time: 196 us -> 192 us (0.980)
  Pallas kernels: 174 us -> 170 us
    pallas_call x1, Pallas kernels: 174 us -> 170 us  [run(): pl.pallas_call(functools.partial(kernel, n, R, oc, lengths, count), out_s...]
    slice x2 -> x0, local copies, waits for them, and re-layouts: 3.73 us -> none  [the longest x1 1.96 us: per_device(): dzv[:, :tv_len].astype(bf16)]
    unnamed x20 -> x22, local copies, waits for them, and re-layouts: 5.87 us -> 9.31 us
where the time goes in v4:
time: 192 us; the launch traced here: 190 us
  Pallas kernels  170 us (89%)
  local copies, waits for them, and re-layouts  12.7 us (7%)
  other arithmetic  6.27 us (3%)
    pallas_call x1, Pallas kernels, run(): pl.pallas_call(functools.partial(kernel, n, R, oc, lengths, count), out_s...  170 us
    unnamed x22, local copies, waits for them, and re-layouts  9.31 us

profile of v4, /device:TPU:13, one launch (start us, length us, event | category | flops | bytes accessed | tf_op | source)
XLA Modules:
  0.0 189.8 jit_solution(6011428829467583282)
XLA Ops:
  0.6 1.3 pad_maximum_fusion.3.gain_ref
  2.0 0.7 multiply_convert_fusion
  2.7 0.0 copy-start.5
  2.7 0.0 copy-start.6
  2.7 0.0 copy-start.7
  2.7 0.9 constant_dynamic-slice_fusion
  3.6 1.0 constant_dynamic-slice_fusion.3
  4.8 0.0 copy-start.3
  4.8 0.0 copy-start.4
  4.8 0.8 pad_maximum_fusion.2.w_ref
  5.6 0.0 copy-done.5
  5.6 0.0 copy-done.6
  5.6 0.0 copy-done.7
  5.7 0.9 pad_maximum_fusion.1.ta_ref
  6.5 0.0 copy-done.3
  6.5 0.0 copy-done.4
  6.5 0.1 fusion.9
  6.6 1.0 pad_maximum_fusion.tv_ref
  7.6 170.1 %shard_map.187 = (bf16[1,196,1024]{2,1,0:T(8,128)(2,1)}, bf16[1,128,1024]{2,1,0:T(8,128)(2,1)}, f32[2,1,8,1024]{3,2,1,0:T(8,128)}, f32[128,3072]{1,0:T(8,128)}, ...) custom-call(bf16[2,128,1024]{2,1,0:T(8,128)(2,1)} %pad_maximum_fusion.2.w_ref, ...), custom_call_target="tpu_custom_call" | custom-call | tf_op jit(solution)/shard_map/pallas_call | solution.py:433
  177.8 1.4 fusion.17
  179.1 1.4 fusion.16
  180.5 1.8 copy.27
  182.3 1.7 copy.28
  184.0 0.0 copy-start.2
  184.0 0.0 copy-start
  184.0 2.8 %copy.29 = f32[128,3072]{1,0:T(8,128)} copy(f32[128,3072]{1,0:T(8,128)} %get-tuple-element.54) | data formatting | bytes 3145728
  186.8 0.0 copy-done.2
  186.8 0.8 copy.30
  187.6 0.0 copy-done
  187.6 0.0 copy-start.1
  187.6 1.1 copy.31
  188.8 0.3 copy-done.1
  189.0 0.8 copy.32
  (3 shorter events, 0.1 us)
Async XLA Ops:
  2.7 2.9 %copy-start.5 = (bf16[1,128,1024]{2,1,0:T(8,128)(2,1)S(1)}, bf16[1,128,1024]{2,1,0:T(8,128)(2,1)}, u32[]{:S(2)}) copy-start(bf16[1,128,1024]{2,1,0:T(8,128)(2,1)} %param.13) | copy-start | bytes 786436
  2.7 2.9 %copy-start.6 = (bf16[1,128,1024]{2,1,0:T(8,128)(2,1)S(1)}, bf16[1,128,1024]{2,1,0:T(8,128)(2,1)}, u32[]{:S(2)}) copy-start(bf16[1,128,1024]{2,1,0:T(8,128)(2,1)} %param.22) | copy-start | bytes 786436
  2.7 2.9 %copy-start.7 = (bf16[1,8,1024]{2,1,0:T(8,128)(2,1)S(1)}, bf16[1,8,1024]{2,1,0:T(8,128)(2,1)}, u32[]{:S(2)}) copy-start(bf16[1,8,1024]{2,1,0:T(8,128)(2,1)} %param.14) | copy-start | bytes 49156
  4.8 1.8 copy-start.3
  4.8 1.8 copy-start.4
  184.0 2.9 %copy-start.2 = (f32[128,1024]{1,0:T(8,128)S(1)}, f32[128,1024]{1,0:T(8,128)}, u32[]{:S(2)}) copy-start(f32[128,1024]{1,0:T(8,128)} %get-tuple-element.55) | copy-start | bytes 1572868
  184.0 3.7 %copy-start = (f32[128,3072]{1,0:T(8,128)S(1)}, f32[128,3072]{1,0:T(8,128)}, u32[]{:S(2)}) copy-start(f32[128,3072]{1,0:T(8,128)} %get-tuple-element.56) | copy-start | bytes 4718596
  187.6 1.4 copy-start.1
